TPU v7x, 32 devices: a whole 2x2x4 slice. The times are simulated.
32 devices in a mesh: les: 8 (over y, x, core), modes: 4 (over z).
Axes of the slice: x: 2, y: 2, z: 4, core: 2. Of those that a mesh axis runs over, the one named last changes fastest.
Arguments:
- pressure: bfloat16 [65536, 512], P('les', 'modes'), may hold values from -6 to 6
- targets: int32 [65536], P('les'), may hold values from 0 to 32767, as said below
- counts: int32 [8], P('les'), may hold values from 1 to 8192, as said below
- pseudo_inverse: bfloat16 [2, 1536, 16384], P(None, None, ('les', 'modes')), may hold values from -0.046875 to 0.046875
Outputs:
- harmonics: float32 [2, 2, 8, 1536], P(None, None, None, ('les', 'modes'))
Inputs may be any that keep to these rules, and one draw needn't show every extreme that they name: `counts`: some partition holds exactly 8192 live faces; all partitions together hold 32768. `targets`: the live slots (slot f of partition i with f < counts[i]) name every station point exactly once. Point p of a station lies in the point rows of les index p // (512 * 4); at most 1024 live faces of one partition lie in the point rows of one les index, and some partition reaches that bound. Slots that are not live hold arbitrary indices in the range.
All inputs are finite; a program needn't handle non-finite values.
Results may differ from a plain program's by a relative error of at most 0.0003.
Values may be sent and summed in bfloat16 or wider, within the bound.
A program may use at most 64 MiB of HBM per device.

v0:
```python
import math

import jax
import jax.numpy as jnp
from jax import lax
from jax.sharding import PartitionSpec as P

TIME = 512
HARM = 8


def fourier_rows():
    sample_ids = jnp.arange(TIME, dtype=jnp.int32)
    orders = jnp.arange(1, HARM + 1, dtype=jnp.int32)
    phase_ids = orders[:, None] * sample_ids[None, :] % TIME
    angles = phase_ids.astype(jnp.float32) * (2.0 * math.pi / TIME)
    scale_factor = math.sqrt(2.0 / TIME)
    return jnp.stack([jnp.cos(angles), -jnp.sin(angles)]) * scale_factor


def rank_by_owner(dest_les, is_live, les_count):
    face_slots = dest_les.shape[0]
    span_width = math.gcd(face_slots, 128)
    owner_ids = jnp.arange(les_count, dtype=jnp.int32)
    matches = ((dest_les[None, :] == owner_ids[:, None]) & is_live[None, :]).astype(jnp.float32)
    matches = matches.reshape(les_count, face_slots // span_width, span_width)
    position = jnp.arange(span_width, dtype=jnp.int32)
    upper = (position[:, None] <= position[None, :]).astype(jnp.float32)
    within = jnp.einsum("nbj,jw->nbw", matches, upper, precision=lax.Precision.HIGHEST)
    block_sums = jnp.sum(matches, axis=2)
    before = jnp.cumsum(block_sums, axis=1) - block_sums
    running = within + before[:, :, None]
    ranked = jnp.sum(running * matches, axis=0).reshape(face_slots) - 1.0
    return ranked.astype(jnp.int32)


def local(pressure, targets, counts, pseudo_inverse):
    les_count = lax.axis_size("les")
    mode_count = lax.axis_size("modes")
    block_len = pressure.shape[1]
    face_slots = targets.shape[0]
    stations = pseudo_inverse.shape[0]
    mode_total = pseudo_inverse.shape[1]
    point_dev = pseudo_inverse.shape[2]
    rows_les = point_dev * mode_count
    points_all = rows_les * les_count
    send_cap = face_slots // les_count
    send_total = les_count * send_cap
    slot_ids = jnp.arange(face_slots, dtype=jnp.int32)
    is_live = slot_ids < counts[0]
    station_of = targets // points_all
    point_of = targets % points_all
    dest_les = point_of // rows_les
    local_row = station_of * rows_les + point_of % rows_les
    face_rank = rank_by_owner(dest_les, is_live, les_count)
    send_pos = jnp.where(is_live, dest_les * send_cap + face_rank, send_total)
    source_face = jnp.full((send_total,), -1, jnp.int32).at[send_pos].set(slot_ids, mode="drop")
    slot_used = source_face >= 0
    source_safe = jnp.maximum(source_face, 0)
    row_tags = jnp.where(slot_used, jnp.take(local_row, source_safe, axis=0), -1).reshape(
        1, send_total
    )
    tags_in = lax.all_to_all(row_tags, "les", split_axis=1, concat_axis=1, tiled=True)
    arrival = jnp.where(tags_in[0] >= 0, tags_in[0], stations * rows_les)
    arrival_ids = jnp.arange(send_total, dtype=jnp.int32)
    arrived_from = (
        jnp.zeros((stations * rows_les,), jnp.int32).at[arrival].set(arrival_ids, mode="drop")
    )
    fourier = fourier_rows()
    block_start = lax.axis_index("modes") * block_len
    block_rows = lax.dynamic_slice_in_dim(fourier, block_start, block_len, 2)
    block_rows = block_rows.reshape(2 * HARM, block_len)
    spectra = lax.dot_general(
        pressure.astype(jnp.float32),
        block_rows,
        (((1,), (1,)), ((), ())),
        precision=lax.Precision.HIGHEST,
    )
    picked = jnp.take(spectra, source_safe, axis=0)
    outgoing = jnp.where(slot_used[:, None], picked, jnp.zeros_like(picked))
    incoming = lax.all_to_all(outgoing, "les", split_axis=0, concat_axis=0, tiled=True)
    gathered = jnp.take(incoming, arrived_from, axis=0)
    gathered = gathered.reshape(stations, rows_les, 2 * HARM)
    summed = lax.psum_scatter(gathered, "modes", scatter_dimension=1, tiled=True)
    partial_value = []
    for station_index in range(stations):
        weights = pseudo_inverse[station_index].astype(jnp.float32)
        projected = lax.dot_general(
            summed[station_index],
            weights,
            (((0,), (1,)), ((), ())),
            precision=lax.Precision.HIGHEST,
        )
        partial_value.append(projected.reshape(2, HARM, mode_total))
    shares = jnp.stack(partial_value)
    return lax.psum_scatter(shares, ("les", "modes"), scatter_dimension=3, tiled=True)


def solution(mesh):
    placed = (P("les", "modes"), P("les"), P("les"), P(None, None, ("les", "modes")))
    return jax.shard_map(
        local,
        mesh=mesh,
        in_specs=placed,
        out_specs=P(None, None, None, ("les", "modes")),
        check_vma=False,
    )
```

profile of v0, /device:TPU:0, one launch (start us, length us, event | category | flops | bytes accessed | tf_op | source)
XLA Modules:
  0.0 323.5 jit_solution(5124301517689672651)
XLA Ops:
  6.5 0.0 copy-start
  7.4 0.8 fusion.13
  8.2 0.1 convert_reduce_fusion
  8.3 0.2 reduce_window_sum.11
  8.6 0.2 fusion.5
  8.8 0.8 compare_select_fusion.2
  9.6 30.5 %scatter_custom_fusion = s32[8192]{0:T(1024)S(1)} fusion(s32[8192]{0:T(1024)S(1)} %compare_select_fusion.2, s32[8192]{0:T(1024)S(1)} %iota.64, s32[]{:T(128)} %constant.117.clone.1), kind=kCustom, calls=%fused_computation.68 | custom fusion | bytes 32772 | tf_op jit(solution)/shard_map/scatter | solution.py:57
  40.1 45.5 %gather_fusion = s32[8192]{0:T(1024)S(1)} fusion(s32[8192]{0:T(1024)S(1)} %get-tuple-element.8, s32[8192]{0:T(1024)S(1)} %maximum_clamp_fusion), kind=kCustom, calls=%fused_computation | custom fusion | bytes 98304 | tf_op jit(solution)/shard_map/jit(_take)/gather | solution.py:60
  85.6 0.6 select_select_fusion.1
  86.3 5.2 %all-to-all-start = ((s32[1,8,1024]{2,0,1:T(1,128)}), s32[1,8,1024]{2,0,1:T(1,128)S(1)}, u32[]{:S(2)}, u32[]{:S(2)}) async-start(s32[1,8,1024]{2,0,1:T(1,128)} %bitcast.4), calls=%async_computation | async-start | bytes 65536 | tf_op jit(solution)/shard_map/all_to_all | solution.py:63
  91.4 0.2 sine_negate_fusion
  91.6 0.0 copy-done
  91.7 1.7 convolution_bitcast_fusion
  93.4 2.6 copy.9
  96.0 29.9 %gather_fusion.1 = f32[8192,16]{1,0:T(8,128)} fusion(f32[8192,16]{1,0:T(8,128)} %copy.9, s32[8192]{0:T(1024)S(1)} %maximum_clamp_fusion), kind=kCustom, calls=%fused_computation.1 | custom fusion | bytes 1081344 | tf_op jit(solution)/shard_map/jit(_take)/gather | solution.py:79
  125.9 2.8 copy.10
  128.7 0.9 select_select_fusion
  129.6 0.0 all-to-all-done
  129.6 4.2 %all-to-all-start.1 = ((f32[8,1024,16]{1,2,0:T(8,128)}), f32[8,1024,16]{1,2,0:T(8,128)S(1)}, u32[]{:S(2)}, u32[]{:S(2)}) async-start(f32[8,1024,16]{1,2,0:T(8,128)} %select_select_fusion), calls=%async_computation.1 | async-start | bytes 1048576 | tf_op jit(solution)/shard_map/all_to_all | solution.py:81
  133.8 0.0 reduce-scatter.5.cloned.1.call-start
  133.8 0.1 compare_select_fusion
  133.9 30.5 %scatter_custom_fusion.1 = s32[4096]{0:T(1024)S(1)} fusion(s32[8192]{0:T(1024)S(1)} %bitcast.62, s32[8192]{0:T(1024)S(1)} %iota.65, s32[]{:T(128)} %constant.116.clone.1), kind=kCustom, calls=%fused_computation.77 | custom fusion | bytes 16388 | tf_op jit(solution)/shard_map/scatter | solution.py:67
  164.4 0.0 all-to-all-done.1
  164.4 2.6 copy.11
  167.0 16.3 %gather_fusion.2 = f32[4096,16]{1,0:T(8,128)} fusion(f32[8192,16]{1,0:T(8,128)} %bitcast.56, s32[4096]{0:T(1024)S(1)} %fusion.27), kind=kCustom, calls=%fused_computation.2 | custom fusion | bytes 540672 | tf_op jit(solution)/shard_map/jit(_take)/gather | solution.py:82
  183.3 2.2 copy.12
  185.4 0.7 broadcast_select_fusion
  186.2 0.0 reduce-scatter.5.cloned.1.call-update
  186.2 0.0 reduce-scatter.7.cloned.1.call-start
  186.2 21.4 %reduce-scatter.5.cloned.1.call-done = f32[2,512,16]{1,2,0:T(8,128)} async-done(((f32[2,2048,16]{1,2,0:T(8,128)}), f32[2,512,16]{1,2,0:T(8,128)}) %reduce-scatter.5.cloned.1.call-update) | async-done | bytes 65552 | tf_op jit(solution)/shard_map/reduce_scatter | solution.py:84
  207.7 2.7 convolution_bitcast_fusion.1
  210.4 2.8 convolution_bitcast_fusion.2
  213.2 3.3 %copy.13 = f32[2,2,8,1536]{2,1,0,3:T(2,128)} copy(f32[2,2,8,1536]{3,2,1,0:T(8,128)S(1)} %pad_maximum_fusion) | data formatting | bytes 393216
  216.5 4.7 %reshape.276 = f32[1536,32]{1,0:T(8,128)} reshape(f32[1536,2,2,8]{3,2,1,0:T(2,128)} %bitcast.58) | data formatting | bytes 393216
  221.2 0.0 reduce-scatter.7.cloned.1.call-update
  221.2 93.9 %reduce-scatter.7.cloned.1.call-done = f32[48,32]{1,0:T(8,128)} async-done(((f32[1536,32]{1,0:T(8,128)}), f32[48,32]{1,0:T(8,128)}) %reduce-scatter.7.cloned.1.call-update) | async-done | bytes 6160
  315.1 0.9 reshape.277
  315.9 0.7 copy.14
  (12 shorter events, 0.1 us)
Async XLA Ops:
  6.5 85.1 %copy-start = (bf16[8192,128]{1,0:T(8,128)(2,1)S(1)}, bf16[8192,128]{1,0:T(8,128)(2,1)}, u32[]{:S(2)}) copy-start(bf16[8192,128]{1,0:T(8,128)(2,1)} %param.4) | copy-start | bytes 6291460
  86.3 43.3 %all-to-all-start = ((s32[1,8,1024]{2,0,1:T(1,128)}), s32[1,8,1024]{2,0,1:T(1,128)S(1)}, u32[]{:S(2)}, u32[]{:S(2)}) async-start(s32[1,8,1024]{2,0,1:T(1,128)} %bitcast.4), calls=%async_computation | async-start | bytes 65536 | tf_op jit(solution)/shard_map/all_to_all | solution.py:63
  129.6 34.8 %all-to-all-start.1 = ((f32[8,1024,16]{1,2,0:T(8,128)}), f32[8,1024,16]{1,2,0:T(8,128)S(1)}, u32[]{:S(2)}, u32[]{:S(2)}) async-start(f32[8,1024,16]{1,2,0:T(8,128)} %select_select_fusion), calls=%async_computation.1 | async-start | bytes 1048576 | tf_op jit(solution)/shard_map/all_to_all | solution.py:81
  133.8 73.9 %reduce-scatter.5.cloned.1.call-start = ((), (), s32[]{:S(2)}) async-start(), calls=%async_computation.4 | async-start | bytes 327680 | tf_op jit(solution)/shard_map/reduce_scatter | solution.py:84
  186.2 128.9 %reduce-scatter.7.cloned.1.call-start = ((), (), s32[]{:S(2)}) async-start(), calls=%async_computation.5 | async-start | bytes 811008
Sparse Core Ops, SparseCore 0:
  186.3 21.3 reduce-scatter.4
  221.3 93.6 reduce-scatter.6
where the time goes:
time: 324 us; the launch traced here: 323 us
  local copies, waits for them, and re-layouts  172 us (53%)
  waiting for transfers between devices  115 us (35%)
  between operations  14.4 us (4%)
  starting transfers between devices  9.44 us (3%)
  matrix products  7.45 us (2%)
  other arithmetic  4.52 us (1%)
    unnamed x3, waiting for transfers between devices  93.9 us
    gather x1, local copies, waits for them, and re-layouts, local(): jnp.take(local_row, source_safe, axis=0)  45.5 us
    gather x2, local copies, waits for them, and re-layouts, local(): picked = jnp.take(spectra, source_safe, axis=0)  32.7 us
    scatter x1, local copies, waits for them, and re-layouts, local(): jnp.full((send_total,), -1, jnp.int32).at[send_pos]  30.5 us
    scatter x1, local copies, waits for them, and re-layouts, local(): jnp.zeros((stations * rows_les,), jnp.int32).at[arrival]  30.5 us
    reduce_scatter x1, waiting for transfers between devices, local(): lax.psum_scatter(gathered, 'modes', scatter_dimension=1, tiled=True)  21.4 us
    gather x2, local copies, waits for them, and re-layouts, local(): gathered = jnp.take(incoming, arrived_from, axis=0)  18.4 us
    unnamed x6, local copies, waits for them, and re-layouts  9.54 us
  transfers between devices with their start and end apart: 4, of which 2 were waited for; matrix products, arithmetic and copies ran while one was open for 21% of the time, Pallas kernels for 0%

commit v1 on v0

v1 whole, which is shorter than its diff:
```python
import functools
import math

import jax
import jax.numpy as jnp
from jax import lax
from jax.experimental import pallas as pl
from jax.experimental.pallas import tpu as pltpu
from jax.sharding import PartitionSpec as P

TIME = 512
HARM = 8
COLS = 2 * HARM
LANES = 128
GROUPS = LANES // COLS
UNROLL = 16
VMEM_BYTES = 56 * 1024 * 1024
MESH = pl.DeviceIdType.MESH


def fourier_rows():
    sample_ids = jnp.arange(TIME, dtype=jnp.int32)
    orders = jnp.arange(1, HARM + 1, dtype=jnp.int32)
    phase_ids = orders[:, None] * sample_ids[None, :] % TIME
    angles = phase_ids.astype(jnp.float32) * (2.0 * math.pi / TIME)
    scale_factor = math.sqrt(2.0 / TIME)
    return jnp.stack([jnp.cos(angles), -jnp.sin(angles)]) * scale_factor


def rank_by_owner(dest_les, is_live, les_count):
    face_slots = dest_les.shape[0]
    span_width = math.gcd(face_slots, 128)
    owner_ids = jnp.arange(les_count, dtype=jnp.int32)
    matches = ((dest_les[None, :] == owner_ids[:, None]) & is_live[None, :]).astype(jnp.float32)
    matches = matches.reshape(les_count, face_slots // span_width, span_width)
    position = jnp.arange(span_width, dtype=jnp.int32)
    upper = (position[:, None] <= position[None, :]).astype(jnp.float32)
    within = jnp.einsum("nbj,jw->nbw", matches, upper, precision=lax.Precision.HIGHEST)
    block_sums = jnp.sum(matches, axis=2)
    before = jnp.cumsum(block_sums, axis=1) - block_sums
    running = within + before[:, :, None]
    ranked = jnp.sum(running * matches, axis=0).reshape(face_slots) - 1.0
    totals = jnp.sum(block_sums, axis=1)
    return ranked.astype(jnp.int32), totals.astype(jnp.int32)


def lane_group(shape):
    return lax.broadcasted_iota(jnp.int32, shape, len(shape) - 1) // COLS


def pack_kernel(counts, pos, rows, pressure, basis, out, tags, spectra, placed):
    face_slots = pressure.shape[0]
    chunk = math.gcd(face_slots, 1024)

    @pl.loop(0, face_slots // chunk)
    def _(step):
        at = pl.ds(pl.multiple_of(step * chunk, chunk), chunk)
        block = pressure[at, :]
        spectra[at, :] = jnp.dot(
            block, basis[0], preferred_element_type=jnp.float32
        ) + jnp.dot(block, basis[1], preferred_element_type=jnp.float32)

    @pl.loop(0, (counts[0] + UNROLL - 1) // UNROLL)
    def _(step):
        base = pl.multiple_of(step * UNROLL, UNROLL)
        for at in range(UNROLL):
            where = pos[base + at]
            placed[pl.ds(where, 1), :] = spectra[pl.ds(base + at, 1), :]
            tags[where] = rows[base + at]

    les_count, rank_rows, _ = out.shape
    group = lane_group((rank_rows, LANES))

    @pl.loop(0, les_count)
    def _(owner):
        total = jnp.zeros((rank_rows, LANES), jnp.float32)
        for part in range(GROUPS):
            start = pl.multiple_of((owner * GROUPS + part) * rank_rows, rank_rows)
            total = jnp.where(group == part, placed[pl.ds(start, rank_rows), :], total)
        out[owner] = total


def unpack_kernel(counts, tags, data, out, spread, placed):
    les_count = data.shape[0]
    mode_count, block_rows, _ = out.shape
    rank_rows = spread.shape[0] // (les_count * GROUPS)
    cap = rank_rows * GROUPS

    @pl.loop(0, les_count)
    def _(source):
        block = data[source, pl.ds(0, rank_rows), :]
        for part in range(GROUPS):
            start = pl.multiple_of(source * cap + part * rank_rows, rank_rows)
            moved = block if part == 0 else pltpu.roll(block, LANES - part * COLS, 1)
            spread[pl.ds(start, rank_rows), :] = moved

    @pl.loop(0, les_count)
    def _(source):
        @pl.loop(0, (counts[source] + UNROLL - 1) // UNROLL)
        def _(step):
            base = pl.multiple_of(source * cap + step * UNROLL, UNROLL)
            for at in range(UNROLL):
                placed[pl.ds(tags[base + at], 1), :] = spread[pl.ds(base + at, 1), :]

    group = lane_group((block_rows, LANES))
    halves = GROUPS // 2

    @pl.loop(0, mode_count)
    def _(mode):
        total = jnp.zeros((block_rows, LANES), jnp.float32)
        for part in range(GROUPS):
            station, piece = part // halves, part % halves
            start = (station * mode_count + mode) * halves * block_rows + piece * block_rows
            block = placed[pl.ds(pl.multiple_of(start, block_rows), block_rows), :]
            moved = block if part == 0 else pltpu.roll(block, part * COLS, 1)
            total = jnp.where(group == part, moved, total)
        out[mode] = total


def tail_kernel(
    les_count, mode_count, blocks, pinv, out,
    weights, recv_modes, shares, recv_all,
    load_sem, mode_send, mode_recv, all_send, all_recv,
):
    les, mode = lax.axis_index("les"), lax.axis_index("modes")
    count = les_count * mode_count
    me = les * mode_count + mode
    load = pltpu.make_async_copy(pinv, weights, load_sem)
    load.start()
    barrier = pltpu.get_barrier_semaphore()

    @pl.loop(1, count)
    def _(step):
        peer = lax.rem(me + step, count)
        pl.semaphore_signal(
            barrier, inc=1, device_id=(peer // mode_count, lax.rem(peer, mode_count)),
            device_id_type=MESH,
        )

    pl.semaphore_wait(barrier, count - 1)
    copies = []
    for step in range(1, mode_count):
        peer = lax.rem(mode + step, mode_count)
        copy = pltpu.make_async_remote_copy(
            src_ref=blocks.at[peer],
            dst_ref=recv_modes.at[step - 1],
            send_sem=mode_send.at[step - 1],
            recv_sem=mode_recv.at[step - 1],
            device_id=(les, peer),
            device_id_type=MESH,
        )
        copy.start()
        copies.append(copy)
    total = blocks[mode]
    for step in range(1, mode_count):
        copies[step - 1].wait()
        total = total + recv_modes[step - 1]
    load.wait()
    turned = total.T
    halves = GROUPS // 2
    width = out.shape[2]
    for station in range(2):
        first = station * halves
        rows = jnp.concatenate(
            [turned[(first + at) * COLS:(first + at + 1) * COLS] for at in range(halves)], axis=1
        )
        high = rows.astype(jnp.bfloat16)
        low = (rows - high.astype(jnp.float32)).astype(jnp.bfloat16)
        both = jnp.concatenate([high, low], axis=0)
        projected = lax.dot_general(
            both, weights[station], (((1,), (1,)), ((), ())), preferred_element_type=jnp.float32
        )
        projected = projected[:COLS] + projected[COLS:]
        lane = station * (LANES // 2)
        for peer in range(count):
            shares[peer, :, lane:lane + width] = projected[:, peer * width:(peer + 1) * width]

    @pl.loop(1, count)
    def _(step):
        peer = lax.rem(me + step, count)
        pltpu.make_async_remote_copy(
            src_ref=shares.at[peer],
            dst_ref=recv_all.at[step - 1],
            send_sem=all_send,
            recv_sem=all_recv,
            device_id=(peer // mode_count, lax.rem(peer, mode_count)),
            device_id_type=MESH,
        ).start()

    pltpu.make_async_copy(recv_all, recv_all, all_recv).wait()
    result = shares[me] + jnp.sum(recv_all[...], axis=0)
    for station in range(2):
        lane = station * (LANES // 2)
        out[station] = result[:, lane:lane + width]
    pltpu.make_async_copy(recv_all, recv_all, all_send).wait()


def local(pressure, targets, counts, pseudo_inverse):
    les_count = lax.axis_size("les")
    mode_count = lax.axis_size("modes")
    block_len = pressure.shape[1]
    face_slots = targets.shape[0]
    stations, mode_total, point_dev = pseudo_inverse.shape
    rows_les = point_dev * mode_count
    points_all = rows_les * les_count
    all_rows = stations * rows_les
    send_cap = face_slots // les_count
    send_total = les_count * send_cap
    rank_rows = send_cap // GROUPS
    block_rows = stations * point_dev // GROUPS
    device_count = les_count * mode_count
    vmem = pl.BlockSpec(memory_space=pltpu.VMEM)
    smem = pl.BlockSpec(memory_space=pltpu.SMEM)

    slot_ids = jnp.arange(face_slots, dtype=jnp.int32)
    is_live = slot_ids < counts[0]
    station_of = targets // points_all
    point_of = targets % points_all
    dest_les = point_of // rows_les
    local_row = station_of * rows_les + point_of % rows_les
    face_rank, totals = rank_by_owner(dest_les, is_live, les_count)
    send_pos = jnp.where(is_live, dest_les * send_cap + face_rank, send_total)

    fourier = fourier_rows()
    block_start = lax.axis_index("modes") * block_len
    basis = lax.dynamic_slice_in_dim(fourier, block_start, block_len, 2)
    basis = basis.reshape(COLS, block_len).T
    basis = jnp.tile(basis, (1, GROUPS))
    high = lax.reduce_precision(basis, 8, 7)
    basis = jnp.stack([high, basis - high]).astype(jnp.bfloat16)

    packed, tags = pl.pallas_call(
        pack_kernel,
        out_shape=(
            jax.ShapeDtypeStruct((les_count, rank_rows, LANES), jnp.float32),
            jax.ShapeDtypeStruct((send_total + LANES,), jnp.int32),
        ),
        in_specs=[smem, smem, smem, vmem, vmem],
        out_specs=(vmem, smem),
        scratch_shapes=[
            pltpu.VMEM((face_slots, LANES), jnp.float32),
            pltpu.VMEM((send_total + 8, LANES), jnp.float32),
        ],
        compiler_params=pltpu.CompilerParams(vmem_limit_bytes=VMEM_BYTES),
        name="pack",
    )(counts, send_pos, local_row, pressure, basis)

    rank_ids = jnp.arange(send_cap, dtype=jnp.int32)
    tags = tags[:send_total].reshape(les_count, send_cap)
    tags = jnp.where(rank_ids[None, :] < totals[:, None], tags, all_rows)
    tags = tags.astype(jnp.float32).reshape(les_count, send_cap // LANES, LANES)
    outgoing = jnp.concatenate([packed, tags], axis=1)
    incoming = lax.all_to_all(outgoing, "les", split_axis=0, concat_axis=0, tiled=True)
    tags_in = incoming[:, rank_rows:].astype(jnp.int32).reshape(les_count, send_cap)
    counts_in = jnp.sum((tags_in < all_rows).astype(jnp.int32), axis=1)

    blocks = pl.pallas_call(
        unpack_kernel,
        out_shape=jax.ShapeDtypeStruct((mode_count, block_rows, LANES), jnp.float32),
        in_specs=[smem, smem, vmem],
        out_specs=vmem,
        scratch_shapes=[
            pltpu.VMEM((send_total, LANES), jnp.float32),
            pltpu.VMEM((all_rows + 8, LANES), jnp.float32),
        ],
        compiler_params=pltpu.CompilerParams(vmem_limit_bytes=VMEM_BYTES),
        name="unpack",
    )(counts_in, tags_in.reshape(send_total), incoming)

    width = mode_total // device_count
    result = pl.pallas_call(
        functools.partial(tail_kernel, les_count, mode_count),
        out_shape=jax.ShapeDtypeStruct((stations, COLS, width), jnp.float32),
        in_specs=[vmem, pl.BlockSpec(memory_space=pl.ANY)],
        out_specs=vmem,
        scratch_shapes=[
            pltpu.VMEM((stations, mode_total, point_dev), jnp.bfloat16),
            pltpu.VMEM((mode_count - 1, block_rows, LANES), jnp.float32),
            pltpu.VMEM((device_count, COLS, LANES), jnp.float32),
            pltpu.VMEM((device_count - 1, COLS, LANES), jnp.float32),
            pltpu.SemaphoreType.DMA,
            pltpu.SemaphoreType.DMA((mode_count - 1,)),
            pltpu.SemaphoreType.DMA((mode_count - 1,)),
            pltpu.SemaphoreType.DMA,
            pltpu.SemaphoreType.DMA,
        ],
        compiler_params=pltpu.CompilerParams(
            collective_id=0, has_side_effects=True, vmem_limit_bytes=VMEM_BYTES
        ),
        name="tail",
    )(blocks, pseudo_inverse)
    return result.reshape(stations, 2, HARM, width)


def solution(mesh):
    placed = (P("les", "modes"), P("les"), P("les"), P(None, None, ("les", "modes")))
    return jax.shard_map(
        local,
        mesh=mesh,
        in_specs=placed,
        out_specs=P(None, None, None, ("les", "modes")),
        check_vma=False,
    )
```

time: 324 us -> 74 us (0.23)
  local copies, waits for them, and re-layouts: 172 us -> 1.42 us
  waiting for transfers between devices: 115 us -> 0 us
  Pallas kernels: 0 us -> 41.4 us
  blocking collectives: 0 us -> 22.4 us
  between operations: 14.4 us -> 0.74 us
  starting transfers between devices: 9.44 us -> 0 us
  matrix products: 7.45 us -> 0.21 us
    gather x5 -> x0, local copies, waits for them, and re-layouts: 96.7 us -> none  [the longest x1 45.5 us: local(): jnp.take(local_row, source_safe, axis=0)]
    unnamed x3 -> x0, waiting for transfers between devices: 93.9 us -> none
    scatter x2 -> x0, local copies, waits for them, and re-layouts: 60.9 us -> none  [the longest x1 30.5 us: local(): jnp.full((send_total,), -1, jnp.int32).at[send_pos]]
    pallas_call x0 -> x3, Pallas kernels: none -> 41.4 us  [the longest x1 21.1 us: local(): pl.pallas_call(functools.partial(tail_kernel, les_count, mode_count), out...]
    all_to_all x0 -> x1, blocking collectives: none -> 22.4 us  [local(): lax.all_to_all(outgoing, 'les', split_axis=0, concat_axis=0, tiled=True)]
    reduce_scatter x1 -> x0, waiting for transfers between devices: 21.4 us -> none  [local(): lax.psum_scatter(gathered, 'modes', scatter_dimension=1, tiled=True)]
    all_to_all x2 -> x0, starting transfers between devices: 9.37 us -> none  [the longest x1 5.17 us: local(): lax.all_to_all(row_tags, 'les', split_axis=1, concat_axis=1, tiled=True)]
    unnamed x6 -> x3, local copies, waits for them, and re-layouts: 9.54 us -> 1.33 us
  transfers between devices with their start and end apart: 4 -> 0, of which waited for: 2 -> 0; matrix products, arithmetic and copies ran while one was open for 21% -> 0% of each run, Pallas kernels for 0% -> 0%
where the time goes in v1:
time: 74 us; the launch traced here: 73.5 us
  Pallas kernels  41.4 us (56%)
  blocking collectives  22.4 us (30%)
  other arithmetic  7.37 us (10%)
  local copies, waits for them, and re-layouts  1.42 us (2%)
  between operations  0.74 us (1%)
    all_to_all x1, blocking collectives, local(): lax.all_to_all(outgoing, 'les', split_axis=0, concat_axis=0, tiled=True)  22.4 us
    pallas_call x1, Pallas kernels, local(): pl.pallas_call(functools.partial(tail_kernel, les_count, mode_count), out...  21.1 us
    pallas_call x1, Pallas kernels, local(): pl.pallas_call(pack_kernel, out_shape=(jax.ShapeDtypeStruct((les_count, r...  11.5 us
    pallas_call x1, Pallas kernels, local(): pl.pallas_call(unpack_kernel, out_shape=jax.ShapeDtypeStruct((mode_count,...  8.76 us

profile of v1, /device:TPU:0, one launch (start us, length us, event | category | flops | bytes accessed | tf_op | source)
XLA Modules:
  0.0 73.5 jit_solution(7805780753322973630)
XLA Ops:
  0.7 0.2 sine_negate_fusion
  0.9 0.1 copy.5
  1.0 1.4 %fusion.10 = (s32[8192]{0:T(1024)}, s32[64,128]{1,0:T(8,128)S(1)}) fusion(s32[8192]{0:T(1024)} %param.5), kind=kLoop, calls=%fused_computation.27 | loop fusion | flops 327680 | bytes 98304 | tf_op jit(solution)/shard_map/add | solution.py:220
  2.4 0.2 convert_reduce_fusion
  2.6 0.2 reduce_window_sum.11
  2.9 0.2 fusion.1
  3.1 0.6 pad_maximum_fusion.1.basis
  3.7 1.4 %fusion.12.pos = s32[8192]{0:T(1024)} fusion(f32[64,128]{1,0:T(8,128)S(1)} %fusion.1, s32[]{:T(128)} %bitcast.22, s32[8192]{0:T(1024)} %param.5), kind=kLoop, calls=%fused_computation.34 | loop fusion | flops 262144 | bytes 98308 | tf_op jit(solution)/shard_map/jit(_where)/select_n | solution.py:222
  5.1 11.5 %pack.1 = (f32[8,128,128]{2,1,0:T(8,128)}, s32[8320]{0:T(1024)}) custom-call(s32[1]{0:T(128)} %copy.8.counts, s32[8192]{0:T(1024)} %fusion.12.pos, s32[8192]{0:T(1024)} %get-tuple-element.13.rows, bf16[8192,128]{1,0:T(8,128)(2,1)} %pressure.1, bf16[2,128,128]{2,1,0:T(8,128)(2,1)} %pad_maximum_fusion.1.basis), custom_call_target="tpu_custom_call" | custom-call | tf_op jit(solution)/shard_map/pack/pallas_call | solution.py:232
  16.6 0.8 %fusion.11 = f32[8,8,128]{2,1,0:T(8,128)S(1)} fusion(s32[8320]{0:T(1024)} %get-tuple-element.8, s32[8,128]{1,0:T(8,128)S(1)} %multiply_add_fusion, s32[8]{0:T(128)S(1)} %convert_element_type.50), kind=kLoop, calls=%fused_computation.32 | loop fusion | flops 24576 | bytes 69664 | tf_op jit(solution)/shard_map/convert_element_type | solution.py:251
  17.5 1.1 %pad_maximum_fusion = f32[8,136,128]{2,1,0:T(8,128)S(1)} fusion(f32[8,8,128]{2,1,0:T(8,128)S(1)} %fusion.11, f32[8,128,128]{2,1,0:T(8,128)} %get-tuple-element.7), kind=kLoop, calls=%fused_computation.3 | loop fusion | flops 139264 | bytes 1114112 | tf_op jit(solution)/shard_map/concatenate | solution.py:252
  18.6 22.4 %all_to_all.5.data = f32[8,136,128]{2,1,0:T(8,128)S(1)} all-to-all(f32[8,136,128]{2,1,0:T(8,128)S(1)} %pad_maximum_fusion), channel_id=1, replica_groups=mesh['les'=8,'modes'=4] {'les'}, dimensions={0} | all-to-all | bytes 1114112 | tf_op jit(solution)/shard_map/all_to_all | solution.py:253
  40.9 0.0 copy-start
  40.9 0.8 %convert_reduce_fusion.2.counts = s32[8]{0:T(128)} fusion(f32[8,136,128]{2,1,0:T(8,128)S(1)} %all_to_all.5.data), kind=kLoop, calls=%fused_computation.35 | loop fusion | flops 32760 | bytes 32800 | tf_op jit(solution)/shard_map/reduce_sum | solution.py:255
  41.7 0.6 fusion.15.tags
  42.3 0.0 copy-done
  42.3 8.8 %unpack.1.blocks = f32[4,128,128]{2,1,0:T(8,128)} custom-call(s32[8]{0:T(128)} %convert_reduce_fusion.2.counts, s32[8192]{0:T(1024)} %fusion.15.tags, f32[8,136,128]{2,1,0:T(8,128)} %copy-done), custom_call_target="tpu_custom_call" | custom-call | tf_op jit(solution)/shard_map/unpack/pallas_call | solution.py:257
  51.0 21.1 %tail.1 = f32[2,16,48]{2,1,0:T(8,128)} custom-call(f32[4,128,128]{2,1,0:T(8,128)} %unpack.1.blocks, bf16[2,1536,512]{2,1,0:T(8,128)(2,1)} %pinv.1), custom_call_target="tpu_custom_call" | custom-call | tf_op jit(solution)/shard_map/tail/pallas_call | solution.py:271
  72.2 1.3 %copy.9 = f32[2,2,8,48]{3,2,1,0:T(8,128)} copy(f32[2,2,8,48]{3,2,1,0:T(8,128)} %bitcast.25) | data formatting | bytes 12288
  (8 shorter events, 0.1 us)
Async XLA Ops:
  40.9 1.4 %copy-start = (f32[8,136,128]{2,1,0:T(8,128)}, f32[8,136,128]{2,1,0:T(8,128)S(1)}, u32[]{:S(2)}) copy-start(f32[8,136,128]{2,1,0:T(8,128)S(1)} %all_to_all.5.data) | copy-start | bytes 1671172

commit v2 on v1

v2 whole, which is shorter than its diff:
```python
import functools
import math

import jax
import jax.numpy as jnp
from jax import lax
from jax.experimental import pallas as pl
from jax.experimental.pallas import tpu as pltpu
from jax.sharding import PartitionSpec as P

TIME = 512
HARM = 8
COLS = 2 * HARM
LANES = 128
GROUPS = LANES // COLS
UNROLL = 16
VMEM_BYTES = 56 * 1024 * 1024
MESH = pl.DeviceIdType.MESH


def fourier_rows():
    sample_ids = jnp.arange(TIME, dtype=jnp.int32)
    orders = jnp.arange(1, HARM + 1, dtype=jnp.int32)
    phase_ids = orders[:, None] * sample_ids[None, :] % TIME
    angles = phase_ids.astype(jnp.float32) * (2.0 * math.pi / TIME)
    scale_factor = math.sqrt(2.0 / TIME)
    return jnp.stack([jnp.cos(angles), -jnp.sin(angles)]) * scale_factor


def lane_group(shape):
    return lax.broadcasted_iota(jnp.int32, shape, len(shape) - 1) // COLS


def pack_kernel(
    rows_les, cap, stride, counts, targets, pressure, basis, out, tags,
    spectra, placed, pos_rows, pos, row_rows, rows, pos_sem, row_sem,
):
    les_count, rank_rows, _ = out.shape
    points_all = rows_les * les_count
    face_slots, block_len = pressure.shape
    lines = targets.shape[0]
    chunk = math.gcd(face_slots, 1024)

    target = targets[...]
    point = target % points_all
    station = target // points_all
    owner_of = point // rows_les
    line = lax.broadcasted_iota(jnp.int32, (lines, LANES), 0)
    lane = lax.broadcasted_iota(jnp.int32, (lines, LANES), 1)
    owner_of = jnp.where(line * LANES + lane < counts[0], owner_of, les_count)
    row_rows[...] = station * rows_les + point % rows_les
    row_copy = pltpu.make_async_copy(row_rows, rows, row_sem)
    row_copy.start()
    first = lax.broadcasted_iota(jnp.int32, (LANES, 2 * LANES), 0)
    second = lax.broadcasted_iota(jnp.int32, (LANES, 2 * LANES), 1)
    upper = ((first <= second) | (second >= LANES)).astype(jnp.bfloat16)
    above = lax.broadcasted_iota(jnp.int32, (lines, lines), 0)
    below = lax.broadcasted_iota(jnp.int32, (lines, lines), 1)
    earlier = (above > below).astype(jnp.bfloat16)
    where = jnp.full((lines, LANES), les_count * stride, jnp.int32)
    for owner in range(les_count):
        chosen = owner_of == owner
        match = jnp.where(chosen, 1.0, 0.0).astype(jnp.bfloat16)
        running = jnp.dot(match, upper, preferred_element_type=jnp.float32)
        within, line_total = running[:, :LANES], running[:, LANES:]
        before = jnp.dot(
            earlier, line_total.astype(jnp.bfloat16), preferred_element_type=jnp.float32
        )
        rank = (within + before).astype(jnp.int32) - 1
        where = jnp.where(chosen, owner * stride + rank, where)
        total = (before + line_total)[lines - 1:lines].astype(jnp.int32)
        pos_rows[lines + owner:lines + owner + 1, :] = total
    pos_rows[:lines, :] = where
    pos_copy = pltpu.make_async_copy(pos_rows, pos, pos_sem)
    pos_copy.start()

    @pl.loop(0, face_slots // chunk)
    def _(step):
        at = pl.ds(pl.multiple_of(step * chunk, chunk), chunk)
        block = pressure[at, :]
        block = jnp.concatenate([block, block], axis=1)
        spectra[at, :] = jnp.dot(block, basis[...], preferred_element_type=jnp.float32)

    row_copy.wait()
    pos_copy.wait()
    steps_line = LANES // UNROLL

    @pl.loop(0, (counts[0] + UNROLL - 1) // UNROLL)
    def _(step):
        base = pl.multiple_of(step * UNROLL, UNROLL)
        line_at = step // steps_line
        lane_at = (step % steps_line) * UNROLL
        for at in range(UNROLL):
            where = pos[line_at, lane_at + at]
            placed[pl.ds(where, 1), :] = spectra[pl.ds(base + at, 1), :]
            tags[where] = rows[line_at, lane_at + at]

    @pl.loop(0, les_count)
    def _(owner):
        tags[owner * stride + cap] = pos[lines + owner, 0]

    group = lane_group((rank_rows, LANES))

    @pl.loop(0, les_count)
    def _(owner):
        total = jnp.zeros((rank_rows, LANES), jnp.float32)
        for part in range(GROUPS):
            start = pl.multiple_of(owner * stride + part * rank_rows, rank_rows)
            total = jnp.where(group == part, placed[pl.ds(start, rank_rows), :], total)
        out[owner] = total


def exchange_kernel(
    les_count, stride, data, tags, data_in, tags_in,
    data_send, data_recv, tags_send, tags_recv, own_sem, own_tags_sem,
):
    les, mode = lax.axis_index("les"), lax.axis_index("modes")
    barrier = pltpu.get_barrier_semaphore()
    for step in range(1, les_count):
        peer = lax.rem(les + step, les_count)
        pl.semaphore_signal(barrier, inc=1, device_id=(peer, mode), device_id_type=MESH)
    own = pltpu.make_async_copy(data.at[les], data_in.at[les], own_sem)
    own_at = pl.ds(pl.multiple_of(les * stride, stride), stride)
    own_tags = pltpu.make_async_copy(tags.at[own_at], tags_in.at[own_at], own_tags_sem)
    own.start()
    own_tags.start()
    pl.semaphore_wait(barrier, les_count - 1)
    copies = []
    for step in range(1, les_count):
        peer = lax.rem(les + step, les_count)
        peer_at = pl.ds(pl.multiple_of(peer * stride, stride), stride)
        copy = pltpu.make_async_remote_copy(
            src_ref=tags.at[peer_at],
            dst_ref=tags_in.at[own_at],
            send_sem=tags_send.at[step - 1],
            recv_sem=tags_recv.at[step - 1],
            device_id=(peer, mode),
            device_id_type=MESH,
        )
        copy.start()
        copies.append(copy)
        copy = pltpu.make_async_remote_copy(
            src_ref=data.at[peer],
            dst_ref=data_in.at[les],
            send_sem=data_send.at[step - 1],
            recv_sem=data_recv.at[step - 1],
            device_id=(peer, mode),
            device_id_type=MESH,
        )
        copy.start()
        copies.append(copy)
    own.wait()
    own_tags.wait()
    for copy in copies:
        copy.wait()


def unpack_kernel(cap, stride, tags, data, out, spread, placed):
    les_count = data.shape[0]
    mode_count, block_rows, _ = out.shape
    rank_rows = spread.shape[0] // (les_count * GROUPS)
    @pl.loop(0, les_count)
    def _(source):
        block = data[source, pl.ds(0, rank_rows), :]
        for part in range(GROUPS):
            start = pl.multiple_of(source * cap + part * rank_rows, rank_rows)
            moved = block if part == 0 else pltpu.roll(block, LANES - part * COLS, 1)
            spread[pl.ds(start, rank_rows), :] = moved

    dump = mode_count * GROUPS * block_rows

    @pl.loop(0, les_count)
    def _(source):
        live = tags[source * stride + cap]

        @pl.loop(0, live // UNROLL)
        def _(step):
            start = pl.multiple_of(step * UNROLL, UNROLL)
            for at in range(UNROLL):
                row = tags[source * stride + start + at]
                placed[pl.ds(row, 1), :] = spread[pl.ds(source * cap + start + at, 1), :]

        @pl.when(live % UNROLL > 0)
        def _():
            start = pl.multiple_of(live // UNROLL * UNROLL, UNROLL)
            base = source * cap + start
            for at in range(UNROLL):
                row = jnp.where(start + at < live, tags[source * stride + start + at], dump)
                placed[pl.ds(row, 1), :] = spread[pl.ds(base + at, 1), :]

    group = lane_group((block_rows, LANES))
    halves = GROUPS // 2

    @pl.loop(0, mode_count)
    def _(mode):
        total = jnp.zeros((block_rows, LANES), jnp.float32)
        for part in range(GROUPS):
            station, piece = part // halves, part % halves
            start = (station * mode_count + mode) * halves * block_rows + piece * block_rows
            block = placed[pl.ds(pl.multiple_of(start, block_rows), block_rows), :]
            moved = block if part == 0 else pltpu.roll(block, part * COLS, 1)
            total = jnp.where(group == part, moved, total)
        out[mode] = total


def tail_kernel(
    les_count, mode_count, blocks, pinv, out,
    weights, recv_modes, shares, recv_les, partial, recv_last, load_sem,
    mode_send, mode_recv, les_send, les_recv, last_send, last_recv,
):
    les, mode = lax.axis_index("les"), lax.axis_index("modes")
    load = pltpu.make_async_copy(pinv, weights, load_sem)
    load.start()
    barrier = pltpu.get_barrier_semaphore()
    for step in range(1, mode_count):
        peer = lax.rem(mode + step, mode_count)
        pl.semaphore_signal(barrier, inc=1, device_id=(les, peer), device_id_type=MESH)
    for step in range(1, les_count):
        peer = lax.rem(les + step, les_count)
        pl.semaphore_signal(barrier, inc=1, device_id=(peer, mode), device_id_type=MESH)
    pl.semaphore_wait(barrier, les_count + mode_count - 2)
    copies = []
    for step in range(1, mode_count):
        peer = lax.rem(mode + step, mode_count)
        copy = pltpu.make_async_remote_copy(
            src_ref=blocks.at[peer],
            dst_ref=recv_modes.at[step - 1],
            send_sem=mode_send.at[step - 1],
            recv_sem=mode_recv.at[step - 1],
            device_id=(les, peer),
            device_id_type=MESH,
        )
        copy.start()
        copies.append(copy)
    total = blocks[mode]
    for step in range(1, mode_count):
        copies[step - 1].wait()
        total = total + recv_modes[step - 1]
    load.wait()
    turned = total.T
    halves = GROUPS // 2
    width = out.shape[2]
    for station in range(2):
        first = station * halves
        rows = jnp.concatenate(
            [turned[(first + at) * COLS:(first + at + 1) * COLS] for at in range(halves)], axis=1
        )
        high = rows.astype(jnp.bfloat16)
        low = (rows - high.astype(jnp.float32)).astype(jnp.bfloat16)
        both = jnp.concatenate([high, low], axis=0)
        projected = lax.dot_general(
            both, weights[station], (((1,), (1,)), ((), ())), preferred_element_type=jnp.float32
        )
        projected = projected[:COLS] + projected[COLS:]
        lane = station * (LANES // 2)
        for peer in range(les_count * mode_count):
            piece = projected[:, peer * width:(peer + 1) * width]
            shares[peer // mode_count, peer % mode_count, :, lane:lane + width] = piece

    copies = []
    for step in range(1, les_count):
        peer = lax.rem(les + step, les_count)
        copy = pltpu.make_async_remote_copy(
            src_ref=shares.at[peer],
            dst_ref=recv_les.at[step - 1],
            send_sem=les_send.at[step - 1],
            recv_sem=les_recv.at[step - 1],
            device_id=(peer, mode),
            device_id_type=MESH,
        )
        copy.start()
        copies.append(copy)
    total = shares[les]
    for step in range(1, les_count):
        copies[step - 1].wait()
        total = total + recv_les[step - 1]
    partial[...] = total
    copies = []
    for step in range(1, mode_count):
        peer = lax.rem(mode + step, mode_count)
        copy = pltpu.make_async_remote_copy(
            src_ref=partial.at[peer],
            dst_ref=recv_last.at[step - 1],
            send_sem=last_send.at[step - 1],
            recv_sem=last_recv.at[step - 1],
            device_id=(les, peer),
            device_id_type=MESH,
        )
        copy.start()
        copies.append(copy)
    result = partial[mode]
    for step in range(1, mode_count):
        copies[step - 1].wait()
        result = result + recv_last[step - 1]
    for station in range(2):
        lane = station * (LANES // 2)
        out[station] = result[:, lane:lane + width]


def local(pressure, targets, counts, pseudo_inverse):
    les_count = lax.axis_size("les")
    mode_count = lax.axis_size("modes")
    block_len = pressure.shape[1]
    face_slots = targets.shape[0]
    stations, mode_total, point_dev = pseudo_inverse.shape
    rows_les = point_dev * mode_count
    all_rows = stations * rows_les
    send_cap = face_slots // les_count
    send_total = les_count * send_cap
    stride = (send_cap // 1024 + 1) * 1024
    lines = face_slots // LANES
    rank_rows = send_cap // GROUPS
    block_rows = stations * point_dev // GROUPS
    device_count = les_count * mode_count
    vmem = pl.BlockSpec(memory_space=pltpu.VMEM)
    smem = pl.BlockSpec(memory_space=pltpu.SMEM)

    fourier = fourier_rows()
    block_start = lax.axis_index("modes") * block_len
    basis = lax.dynamic_slice_in_dim(fourier, block_start, block_len, 2)
    basis = basis.reshape(COLS, block_len).T
    basis = jnp.tile(basis, (1, GROUPS))
    high = lax.reduce_precision(basis, 8, 7)
    basis = jnp.concatenate([high, basis - high]).astype(jnp.bfloat16)

    packed, tags = pl.pallas_call(
        functools.partial(pack_kernel, rows_les, send_cap, stride),
        out_shape=(
            jax.ShapeDtypeStruct((les_count, rank_rows, LANES), jnp.float32),
            jax.ShapeDtypeStruct(((les_count + 1) * stride,), jnp.int32),
        ),
        in_specs=[smem, vmem, vmem, vmem],
        out_specs=(vmem, smem),
        scratch_shapes=[
            pltpu.VMEM((face_slots, LANES), jnp.float32),
            pltpu.VMEM((les_count * stride + 8, LANES), jnp.float32),
            pltpu.VMEM((lines + les_count, LANES), jnp.int32),
            pltpu.SMEM((lines + les_count, LANES), jnp.int32),
            pltpu.VMEM((lines, LANES), jnp.int32),
            pltpu.SMEM((lines, LANES), jnp.int32),
            pltpu.SemaphoreType.DMA,
            pltpu.SemaphoreType.DMA,
        ],
        compiler_params=pltpu.CompilerParams(vmem_limit_bytes=VMEM_BYTES),
        name="pack",
    )(counts, targets.reshape(lines, LANES), pressure, basis)

    hbm = pl.BlockSpec(memory_space=pl.ANY)
    peers = les_count - 1
    data_in, tags_in = pl.pallas_call(
        functools.partial(exchange_kernel, les_count, stride),
        out_shape=(
            jax.ShapeDtypeStruct((les_count, rank_rows, LANES), jnp.float32),
            jax.ShapeDtypeStruct((les_count * stride,), jnp.int32),
        ),
        in_specs=[hbm, hbm],
        out_specs=(hbm, hbm),
        scratch_shapes=[pltpu.SemaphoreType.DMA((peers,))] * 4 + [pltpu.SemaphoreType.DMA] * 2,
        compiler_params=pltpu.CompilerParams(collective_id=1, has_side_effects=True),
        name="exchange",
    )(packed, tags)

    blocks = pl.pallas_call(
        functools.partial(unpack_kernel, send_cap, stride),
        out_shape=jax.ShapeDtypeStruct((mode_count, block_rows, LANES), jnp.float32),
        in_specs=[smem, vmem],
        out_specs=vmem,
        scratch_shapes=[
            pltpu.VMEM((send_total, LANES), jnp.float32),
            pltpu.VMEM((all_rows + 8, LANES), jnp.float32),
        ],
        compiler_params=pltpu.CompilerParams(vmem_limit_bytes=VMEM_BYTES),
        name="unpack",
    )(tags_in, data_in)

    width = mode_total // device_count
    result = pl.pallas_call(
        functools.partial(tail_kernel, les_count, mode_count),
        out_shape=jax.ShapeDtypeStruct((stations, COLS, width), jnp.float32),
        in_specs=[vmem, pl.BlockSpec(memory_space=pl.ANY)],
        out_specs=vmem,
        scratch_shapes=[
            pltpu.VMEM((stations, mode_total, point_dev), jnp.bfloat16),
            pltpu.VMEM((mode_count - 1, block_rows, LANES), jnp.float32),
            pltpu.VMEM((les_count, mode_count, COLS, LANES), jnp.float32),
            pltpu.VMEM((les_count - 1, mode_count, COLS, LANES), jnp.float32),
            pltpu.VMEM((mode_count, COLS, LANES), jnp.float32),
            pltpu.VMEM((mode_count - 1, COLS, LANES), jnp.float32),
            pltpu.SemaphoreType.DMA,
            pltpu.SemaphoreType.DMA((mode_count - 1,)),
            pltpu.SemaphoreType.DMA((mode_count - 1,)),
            pltpu.SemaphoreType.DMA((les_count - 1,)),
            pltpu.SemaphoreType.DMA((les_count - 1,)),
            pltpu.SemaphoreType.DMA((mode_count - 1,)),
            pltpu.SemaphoreType.DMA((mode_count - 1,)),
        ],
        compiler_params=pltpu.CompilerParams(
            collective_id=0, has_side_effects=True, vmem_limit_bytes=VMEM_BYTES
        ),
        name="tail",
    )(blocks, pseudo_inverse)
    return result.reshape(stations, 2, HARM, width)


def solution(mesh):
    placed = (P("les", "modes"), P("les"), P("les"), P(None, None, ("les", "modes")))
    return jax.shard_map(
        local,
        mesh=mesh,
        in_specs=placed,
        out_specs=P(None, None, None, ("les", "modes")),
        check_vma=False,
    )
```

time: 74 us -> 81.5 us (1.10)
  Pallas kernels: 41.4 us -> 77.5 us
  blocking collectives: 22.4 us -> 0 us
  other arithmetic: 7.37 us -> 0.81 us
    pallas_call x2 -> x3, Pallas kernels: 20.3 us -> 55.5 us  [the longest x1 26.8 us: local(): pl.pallas_call(functools.partial(exchange_kernel, les_count, stride), out...]
    all_to_all x1 -> x0, blocking collectives: 22.4 us -> none  [local(): lax.all_to_all(outgoing, 'les', split_axis=0, concat_axis=0, tiled=True)]
    another operation x4 -> x1, other arithmetic: 1.47 us -> 0.02 us  [the longest x1 0.63 us: local(): basis = jnp.stack([high, basis - high]).astype(jnp.bfloat16)]
    add x1 -> x0, other arithmetic: 1.43 us -> none  [local(): local_row = station_of * rows_les + point_of % rows_les]
    select_n x1 -> x0, other arithmetic: 1.4 us -> none  [local(): send_pos = jnp.where(is_live, dest_les * send_cap + face_rank, send_total)]
    reduce_sum x2 -> x0, other arithmetic: 0.95 us -> none  [the longest x1 0.75 us: local(): counts_in = jnp.sum((tags_in < all_rows).astype(jnp.int32), axis=1)]
    pallas_call x1, Pallas kernels: 21.1 us -> 22 us  [local(): pl.pallas_call(functools.partial(tail_kernel, les_count, mode_count), out...]
    convert_element_type x2 -> x0, other arithmetic: 0.84 us -> none  [the longest x1 0.83 us: local(): tags = tags.astype(jnp.float32).reshape(les_count, send_cap // LANES, LANES)]
where the time goes in v2:
time: 81.5 us; the launch traced here: 80.5 us
  Pallas kernels  77.5 us (95%)
  local copies, waits for them, and re-layouts  1.42 us (2%)
    pallas_call x1, Pallas kernels, local(): pl.pallas_call(functools.partial(exchange_kernel, les_count, stride), out...  26.8 us
    pallas_call x1, Pallas kernels, local(): pl.pallas_call(functools.partial(tail_kernel, les_count, mode_count), out...  22 us
    pallas_call x1, Pallas kernels, local(): pl.pallas_call(functools.partial(pack_kernel, rows_les, send_cap, stride)...  19.2 us
    pallas_call x1, Pallas kernels, local(): pl.pallas_call(functools.partial(unpack_kernel, send_cap, stride), out_sh...  9.54 us

profile of v2, /device:TPU:0, one launch (start us, length us, event | category | flops | bytes accessed | tf_op | source)
XLA Modules:
  0.0 80.5 jit_solution(12183886288512736592)
XLA Ops:
  0.7 0.2 sine_negate_fusion
  0.9 0.1 copy.5
  1.0 0.6 pad_maximum_fusion.basis
  1.6 19.2 %pack.1 = (f32[8,128,128]{2,1,0:T(8,128)}, s32[18432]{0:T(1024)}) custom-call(s32[1]{0:T(128)S(6)} %copy.8.counts, s32[64,128]{1,0:T(8,128)} %bitcast.9, bf16[8192,128]{1,0:T(8,128)(2,1)} %pressure.1, bf16[256,128]{1,0:T(8,128)(2,1)} %pad_maximum_fusion.basis), custom_call_target="tpu_custom_call" | custom-call | tf_op jit(solution)/shard_map/pack/pallas_call | solution.py:326
  20.8 26.8 %exchange.1 = (f32[8,128,128]{2,1,0:T(8,128)}, s32[16384]{0:T(1024)}) custom-call(f32[8,128,128]{2,1,0:T(8,128)} %get-tuple-element.9.data, s32[18432]{0:T(1024)} %get-tuple-element.10.tags), custom_call_target="tpu_custom_call" | custom-call | tf_op jit(solution)/shard_map/exchange/pallas_call | solution.py:350
  47.6 9.5 %unpack.1.blocks = f32[4,128,128]{2,1,0:T(8,128)} custom-call(s32[16384]{0:T(1024)} %get-tuple-element.11.tags, f32[8,128,128]{2,1,0:T(8,128)} %get-tuple-element.12.data), custom_call_target="tpu_custom_call" | custom-call | tf_op jit(solution)/shard_map/unpack/pallas_call | solution.py:363
  57.2 22.0 %tail.1 = f32[2,16,48]{2,1,0:T(8,128)} custom-call(f32[4,128,128]{2,1,0:T(8,128)} %unpack.1.blocks, bf16[2,1536,512]{2,1,0:T(8,128)(2,1)} %pinv.1), custom_call_target="tpu_custom_call" | custom-call | tf_op jit(solution)/shard_map/tail/pallas_call | solution.py:377
  79.1 1.3 %copy.9 = f32[2,2,8,48]{3,2,1,0:T(8,128)} copy(f32[2,2,8,48]{3,2,1,0:T(8,128)} %bitcast.8) | data formatting | bytes 12288
  (4 shorter events, 0.0 us)

commit v3 on v2

--- a/solution.py
+++ b/solution.py
@@ -3,6 +3,7 @@
 
 import jax
 import jax.numpy as jnp
+import numpy as np
 from jax import lax
 from jax.experimental import pallas as pl
 from jax.experimental.pallas import tpu as pltpu
@@ -18,13 +19,14 @@
 MESH = pl.DeviceIdType.MESH
 
 
-def fourier_rows():
-    sample_ids = jnp.arange(TIME, dtype=jnp.int32)
-    orders = jnp.arange(1, HARM + 1, dtype=jnp.int32)
-    phase_ids = orders[:, None] * sample_ids[None, :] % TIME
-    angles = phase_ids.astype(jnp.float32) * (2.0 * math.pi / TIME)
-    scale_factor = math.sqrt(2.0 / TIME)
-    return jnp.stack([jnp.cos(angles), -jnp.sin(angles)]) * scale_factor
+def fourier_columns():
+    phase_ids = np.arange(TIME)[:, None] * np.arange(1, HARM + 1)[None, :] % TIME
+    angles = phase_ids * (2.0 * math.pi / TIME)
+    columns = np.concatenate([np.cos(angles), -np.sin(angles)], axis=1) * math.sqrt(2.0 / TIME)
+    columns = np.tile(columns, (1, GROUPS)).astype(np.float32)
+    high = columns.astype(jnp.bfloat16)
+    low = (columns - high.astype(np.float32)).astype(jnp.bfloat16)
+    return np.stack([high, low])
 
 
 def lane_group(shape):
@@ -32,7 +34,7 @@
 
 
 def pack_kernel(
-    rows_les, cap, stride, counts, targets, pressure, basis, out, tags,
+    rows_les, cap, stride, counts, mode_at, targets, pressure, basis, out, tags,
     spectra, placed, pos_rows, pos, row_rows, rows, pos_sem, row_sem,
 ):
     les_count, rank_rows, _ = out.shape
@@ -74,26 +76,30 @@
     pos_copy = pltpu.make_async_copy(pos_rows, pos, pos_sem)
     pos_copy.start()
 
+    times = pl.ds(pl.multiple_of(mode_at[0] * block_len, block_len), block_len)
+    block_basis = jnp.concatenate([basis[0, times, :], basis[1, times, :]], axis=0)
+
     @pl.loop(0, face_slots // chunk)
     def _(step):
         at = pl.ds(pl.multiple_of(step * chunk, chunk), chunk)
         block = pressure[at, :]
         block = jnp.concatenate([block, block], axis=1)
-        spectra[at, :] = jnp.dot(block, basis[...], preferred_element_type=jnp.float32)
+        spectra[at, :] = jnp.dot(block, block_basis, preferred_element_type=jnp.float32)
 
     row_copy.wait()
     pos_copy.wait()
-    steps_line = LANES // UNROLL
-
-    @pl.loop(0, (counts[0] + UNROLL - 1) // UNROLL)
-    def _(step):
-        base = pl.multiple_of(step * UNROLL, UNROLL)
-        line_at = step // steps_line
-        lane_at = (step % steps_line) * UNROLL
-        for at in range(UNROLL):
-            where = pos[line_at, lane_at + at]
-            placed[pl.ds(where, 1), :] = spectra[pl.ds(base + at, 1), :]
-            tags[where] = rows[line_at, lane_at + at]
+
+    @pl.loop(0, (counts[0] + LANES - 1) // LANES)
+    def _(line_at):
+        base = pl.multiple_of(line_at * LANES, LANES)
+        for first in range(0, LANES, UNROLL):
+            span = range(first, first + UNROLL)
+            wheres = [pos[line_at, at] for at in span]
+            names = [rows[line_at, at] for at in span]
+            values = [spectra[pl.ds(base + at, 1), :] for at in span]
+            for where, name, value in zip(wheres, names, values):
+                placed[pl.ds(where, 1), :] = value
+                tags[where] = name
 
     @pl.loop(0, les_count)
     def _(owner):
@@ -176,9 +182,11 @@
         @pl.loop(0, live // UNROLL)
         def _(step):
             start = pl.multiple_of(step * UNROLL, UNROLL)
-            for at in range(UNROLL):
-                row = tags[source * stride + start + at]
-                placed[pl.ds(row, 1), :] = spread[pl.ds(source * cap + start + at, 1), :]
+            base = source * cap + start
+            names = [tags[source * stride + start + at] for at in range(UNROLL)]
+            values = [spread[pl.ds(base + at, 1), :] for at in range(UNROLL)]
+            for name, value in zip(names, values):
+                placed[pl.ds(name, 1), :] = value
 
         @pl.when(live % UNROLL > 0)
         def _():
@@ -203,9 +211,14 @@
         out[mode] = total
 
 
+def share_form(width):
+    pieces = 3 if width % 24 == 0 else 1
+    return pieces, width // pieces
+
+
 def tail_kernel(
     les_count, mode_count, blocks, pinv, out,
-    weights, recv_modes, shares, recv_les, partial, recv_last, load_sem,
+    weights, whole, recv_modes, shares, recv_les, partial, recv_last, load_sem,
     mode_send, mode_recv, les_send, les_recv, last_send, last_recv,
 ):
     les, mode = lax.axis_index("les"), lax.axis_index("modes")
@@ -237,25 +250,35 @@
         copies[step - 1].wait()
         total = total + recv_modes[step - 1]
     load.wait()
-    turned = total.T
     halves = GROUPS // 2
     width = out.shape[2]
+    high = total.astype(jnp.bfloat16).astype(jnp.float32)
+    low = total - high
+    lane = lax.broadcasted_iota(jnp.int32, total.shape, 1)
+    projected = []
     for station in range(2):
-        first = station * halves
-        rows = jnp.concatenate(
-            [turned[(first + at) * COLS:(first + at + 1) * COLS] for at in range(halves)], axis=1
-        )
-        high = rows.astype(jnp.bfloat16)
-        low = (rows - high.astype(jnp.float32)).astype(jnp.bfloat16)
-        both = jnp.concatenate([high, low], axis=0)
-        projected = lax.dot_general(
-            both, weights[station], (((1,), (1,)), ((), ())), preferred_element_type=jnp.float32
-        )
-        projected = projected[:COLS] + projected[COLS:]
-        lane = station * (LANES // 2)
-        for peer in range(les_count * mode_count):
-            piece = projected[:, peer * width:(peer + 1) * width]
-            shares[peer // mode_count, peer % mode_count, :, lane:lane + width] = piece
+        rows = []
+        for at in range(halves):
+            shift = LANES - (station * halves + at) * COLS
+            high_at = pltpu.roll(high, shift % LANES, 1)
+            low_at = pltpu.roll(low, (shift + COLS) % LANES, 1)
+            both = jnp.where(lane < COLS, high_at, jnp.where(lane < 2 * COLS, low_at, 0.0))
+            rows.append(both.astype(jnp.bfloat16))
+        result = jnp.dot(
+            weights[station], jnp.concatenate(rows, axis=0), preferred_element_type=jnp.float32
+        )
+        projected.append(result + pltpu.roll(result, LANES - COLS, 1))
+    lane = lax.broadcasted_iota(jnp.int32, projected[0].shape, 1)
+    second = pltpu.roll(projected[1], COLS, 1)
+    both = jnp.where(lane < COLS, projected[0], second)
+    whole[...] = jnp.where(lane < 2 * COLS, both, 0.0)
+    pieces, piece_rows = share_form(width)
+    for peer in range(les_count * mode_count):
+        piece = whole[pl.ds(peer * width, piece_rows), :]
+        for at in range(1, pieces):
+            start = peer * width + at * piece_rows
+            piece = piece + pltpu.roll(whole[pl.ds(start, piece_rows), :], at * 2 * COLS, 1)
+        shares[peer // mode_count, peer % mode_count, pl.ds(0, piece_rows), :] = piece
 
     copies = []
     for step in range(1, les_count):
@@ -292,15 +315,17 @@
     for step in range(1, mode_count):
         copies[step - 1].wait()
         result = result + recv_last[step - 1]
+    turned = result.T
     for station in range(2):
-        lane = station * (LANES // 2)
-        out[station] = result[:, lane:lane + width]
+        for at in range(pieces):
+            start = (at * 2 + station) * COLS
+            piece = turned[start:start + COLS, :piece_rows]
+            out[station, :, at * piece_rows:(at + 1) * piece_rows] = piece
 
 
 def local(pressure, targets, counts, pseudo_inverse):
     les_count = lax.axis_size("les")
     mode_count = lax.axis_size("modes")
-    block_len = pressure.shape[1]
     face_slots = targets.shape[0]
     stations, mode_total, point_dev = pseudo_inverse.shape
     rows_les = point_dev * mode_count
@@ -315,13 +340,7 @@
     vmem = pl.BlockSpec(memory_space=pltpu.VMEM)
     smem = pl.BlockSpec(memory_space=pltpu.SMEM)
 
-    fourier = fourier_rows()
-    block_start = lax.axis_index("modes") * block_len
-    basis = lax.dynamic_slice_in_dim(fourier, block_start, block_len, 2)
-    basis = basis.reshape(COLS, block_len).T
-    basis = jnp.tile(basis, (1, GROUPS))
-    high = lax.reduce_precision(basis, 8, 7)
-    basis = jnp.concatenate([high, basis - high]).astype(jnp.bfloat16)
+    mode_at = lax.axis_index("modes").astype(jnp.int32).reshape(1)
 
     packed, tags = pl.pallas_call(
         functools.partial(pack_kernel, rows_les, send_cap, stride),
@@ -329,7 +348,7 @@
             jax.ShapeDtypeStruct((les_count, rank_rows, LANES), jnp.float32),
             jax.ShapeDtypeStruct(((les_count + 1) * stride,), jnp.int32),
         ),
-        in_specs=[smem, vmem, vmem, vmem],
+        in_specs=[smem, smem, vmem, vmem, vmem],
         out_specs=(vmem, smem),
         scratch_shapes=[
             pltpu.VMEM((face_slots, LANES), jnp.float32),
@@ -343,7 +362,7 @@
         ],
         compiler_params=pltpu.CompilerParams(vmem_limit_bytes=VMEM_BYTES),
         name="pack",
-    )(counts, targets.reshape(lines, LANES), pressure, basis)
+    )(counts, mode_at, targets.reshape(lines, LANES), pressure, jnp.asarray(fourier_columns()))
 
     hbm = pl.BlockSpec(memory_space=pl.ANY)
     peers = les_count - 1
@@ -374,6 +393,7 @@
     )(tags_in, data_in)
 
     width = mode_total // device_count
+    share_rows = (share_form(width)[1] + 7) // 8 * 8
     result = pl.pallas_call(
         functools.partial(tail_kernel, les_count, mode_count),
         out_shape=jax.ShapeDtypeStruct((stations, COLS, width), jnp.float32),
@@ -381,11 +401,12 @@
         out_specs=vmem,
         scratch_shapes=[
             pltpu.VMEM((stations, mode_total, point_dev), jnp.bfloat16),
+            pltpu.VMEM((mode_total, LANES), jnp.float32),
             pltpu.VMEM((mode_count - 1, block_rows, LANES), jnp.float32),
-            pltpu.VMEM((les_count, mode_count, COLS, LANES), jnp.float32),
-            pltpu.VMEM((les_count - 1, mode_count, COLS, LANES), jnp.float32),
-            pltpu.VMEM((mode_count, COLS, LANES), jnp.float32),
-            pltpu.VMEM((mode_count - 1, COLS, LANES), jnp.float32),
+            pltpu.VMEM((les_count, mode_count, share_rows, LANES), jnp.float32),
+            pltpu.VMEM((les_count - 1, mode_count, share_rows, LANES), jnp.float32),
+            pltpu.VMEM((mode_count, share_rows, LANES), jnp.float32),
+            pltpu.VMEM((mode_count - 1, share_rows, LANES), jnp.float32),
             pltpu.SemaphoreType.DMA,
             pltpu.SemaphoreType.DMA((mode_count - 1,)),
             pltpu.SemaphoreType.DMA((mode_count - 1,)),

time: 81.5 us -> 66.6 us (0.82)
  Pallas kernels: 77.5 us -> 63.5 us
    pallas_call x1, Pallas kernels: 26.8 us -> 18.5 us  [local(): pl.pallas_call(functools.partial(exchange_kernel, les_count, stride), out...]
    pallas_call x1, Pallas kernels: 19.2 us -> 12.9 us  [local(): pl.pallas_call(functools.partial(pack_kernel, rows_les, send_cap, stride)...]
where the time goes in v3:
time: 66.6 us; the launch traced here: 65.5 us
  Pallas kernels  63.5 us (95%)
  local copies, waits for them, and re-layouts  1.32 us (2%)
  between operations  0.68 us (1%)
    pallas_call x1, Pallas kernels, local(): pl.pallas_call(functools.partial(tail_kernel, les_count, mode_count), out...  22.5 us
    pallas_call x1, Pallas kernels, local(): pl.pallas_call(functools.partial(exchange_kernel, les_count, stride), out...  18.5 us
    pallas_call x1, Pallas kernels, local(): pl.pallas_call(functools.partial(pack_kernel, rows_les, send_cap, stride)...  12.9 us
    pallas_call x1, Pallas kernels, local(): pl.pallas_call(functools.partial(unpack_kernel, send_cap, stride), out_sh...  9.53 us

profile of v3, /device:TPU:0, one launch (start us, length us, event | category | flops | bytes accessed | tf_op | source)
XLA Modules:
  0.0 65.5 jit_solution(8020671590272742501)
XLA Ops:
  0.7 12.9 %pack.1 = (f32[8,128,128]{2,1,0:T(8,128)}, s32[18432]{0:T(1024)}) custom-call(s32[1]{0:T(128)S(6)} %copy.7.counts, s32[1]{0:T(128)} %bitcast.mode_at, s32[64,128]{1,0:T(8,128)} %bitcast.4, bf16[8192,128]{1,0:T(8,128)(2,1)} %pressure.1, bf16[2,512,128]{2,1,0:T(8,128)(2,1)} %constant.6.clone.basis), custom_call_target="tpu_custom_call" | custom-call | tf_op jit(solution)/shard_map/pack/pallas_call | solution.py:345
  13.6 18.5 %exchange.1 = (f32[8,128,128]{2,1,0:T(8,128)}, s32[16384]{0:T(1024)}) custom-call(f32[8,128,128]{2,1,0:T(8,128)} %get-tuple-element.9.data, s32[18432]{0:T(1024)} %get-tuple-element.10.tags), custom_call_target="tpu_custom_call" | custom-call | tf_op jit(solution)/shard_map/exchange/pallas_call | solution.py:369
  32.1 9.5 %unpack.1.blocks = f32[4,128,128]{2,1,0:T(8,128)} custom-call(s32[16384]{0:T(1024)} %get-tuple-element.11.tags, f32[8,128,128]{2,1,0:T(8,128)} %get-tuple-element.12.data), custom_call_target="tpu_custom_call" | custom-call | tf_op jit(solution)/shard_map/unpack/pallas_call | solution.py:382
  41.6 22.5 %tail.1 = f32[2,16,48]{2,1,0:T(8,128)} custom-call(f32[4,128,128]{2,1,0:T(8,128)} %unpack.1.blocks, bf16[2,1536,512]{2,1,0:T(8,128)(2,1)} %pinv.1), custom_call_target="tpu_custom_call" | custom-call | tf_op jit(solution)/shard_map/tail/pallas_call | solution.py:397
  64.1 1.3 %copy.8 = f32[2,2,8,48]{3,2,1,0:T(8,128)} copy(f32[2,2,8,48]{3,2,1,0:T(8,128)} %bitcast.3) | data formatting | bytes 12288

commit v4 on v3

--- a/solution.py
+++ b/solution.py
@@ -33,15 +33,11 @@
     return lax.broadcasted_iota(jnp.int32, shape, len(shape) - 1) // COLS
 
 
-def pack_kernel(
-    rows_les, cap, stride, counts, mode_at, targets, pressure, basis, out, tags,
-    spectra, placed, pos_rows, pos, row_rows, rows, pos_sem, row_sem,
-):
-    les_count, rank_rows, _ = out.shape
+def index_kernel(rows_les, les_count, counts, targets, sources, tags, wheres, names):
     points_all = rows_les * les_count
-    face_slots, block_len = pressure.shape
     lines = targets.shape[0]
-    chunk = math.gcd(face_slots, 1024)
+    send_lines = sources.shape[0]
+    stride = send_lines // les_count * LANES
 
     target = targets[...]
     point = target % points_all
@@ -50,9 +46,7 @@
     line = lax.broadcasted_iota(jnp.int32, (lines, LANES), 0)
     lane = lax.broadcasted_iota(jnp.int32, (lines, LANES), 1)
     owner_of = jnp.where(line * LANES + lane < counts[0], owner_of, les_count)
-    row_rows[...] = station * rows_les + point % rows_les
-    row_copy = pltpu.make_async_copy(row_rows, rows, row_sem)
-    row_copy.start()
+    names[...] = station * rows_les + point % rows_les + 1
     first = lax.broadcasted_iota(jnp.int32, (LANES, 2 * LANES), 0)
     second = lax.broadcasted_iota(jnp.int32, (LANES, 2 * LANES), 1)
     upper = ((first <= second) | (second >= LANES)).astype(jnp.bfloat16)
@@ -70,13 +64,57 @@
         )
         rank = (within + before).astype(jnp.int32) - 1
         where = jnp.where(chosen, owner * stride + rank, where)
-        total = (before + line_total)[lines - 1:lines].astype(jnp.int32)
-        pos_rows[lines + owner:lines + owner + 1, :] = total
-    pos_rows[:lines, :] = where
-    pos_copy = pltpu.make_async_copy(pos_rows, pos, pos_sem)
-    pos_copy.start()
-
-    times = pl.ds(pl.multiple_of(mode_at[0] * block_len, block_len), block_len)
+    wheres[...] = where
+
+    line_ids = lax.broadcasted_iota(jnp.int32, (send_lines, LANES), 0)
+    lane_ids = lax.broadcasted_iota(jnp.int32, (LANES, LANES), 0)
+    face_lane = lax.broadcasted_iota(jnp.int32, (LANES, LANES), 1).astype(jnp.float32)
+
+    def add_lines(step, total):
+        lefts, rights = [], []
+        for at in range(8):
+            line_at = step * 8 + at
+            where = wheres[pl.ds(line_at, 1), :]
+            name = names[pl.ds(line_at, 1), :]
+            left = jnp.where(line_ids == where // LANES, 1.0, 0.0).astype(jnp.bfloat16)
+            hit = lane_ids == where % LANES
+            face_line = jnp.full((1, LANES), line_at, jnp.int32).astype(jnp.float32)
+            parts = [
+                jnp.where(hit, face_line, 0.0),
+                jnp.where(hit, face_lane, 0.0),
+                jnp.where(hit, (name // 64).astype(jnp.float32), 0.0),
+                jnp.where(hit, (name % 64).astype(jnp.float32), 0.0),
+            ]
+            lefts.append(left)
+            rights.append(jnp.concatenate(parts, axis=0).astype(jnp.bfloat16))
+        return total + lax.dot_general(
+            jnp.concatenate(lefts, axis=1),
+            jnp.concatenate(rights, axis=1),
+            (((1,), (1,)), ((), ())),
+            preferred_element_type=jnp.float32,
+        )
+
+    total = lax.fori_loop(
+        0, lines // 8, add_lines, jnp.zeros((send_lines, 4 * LANES), jnp.float32)
+    )
+    source = total[:, :LANES] * LANES + total[:, LANES:2 * LANES]
+    sources[...] = source.astype(jnp.int32)
+    tags[...] = total[:, 2 * LANES:3 * LANES] * 64 + total[:, 3 * LANES:]
+
+
+def exchange_kernel(
+    les_count, mode_count, sources, tags, pressure, basis, data_in,
+    spectra, placed, packed, send_sem, recv_sem, own_sem,
+):
+    les, mode = lax.axis_index("les"), lax.axis_index("modes")
+    barrier = pltpu.get_barrier_semaphore()
+    for step in range(1, les_count):
+        peer = lax.rem(les + step, les_count)
+        pl.semaphore_signal(barrier, inc=1, device_id=(peer, mode), device_id_type=MESH)
+
+    face_slots, block_len = pressure.shape
+    chunk = math.gcd(face_slots, 1024)
+    times = pl.ds(pl.multiple_of(mode * block_len, block_len), block_len)
     block_basis = jnp.concatenate([basis[0, times, :], basis[1, times, :]], axis=0)
 
     @pl.loop(0, face_slots // chunk)
@@ -86,85 +124,78 @@
         block = jnp.concatenate([block, block], axis=1)
         spectra[at, :] = jnp.dot(block, block_basis, preferred_element_type=jnp.float32)
 
-    row_copy.wait()
-    pos_copy.wait()
-
-    @pl.loop(0, (counts[0] + LANES - 1) // LANES)
-    def _(line_at):
-        base = pl.multiple_of(line_at * LANES, LANES)
-        for first in range(0, LANES, UNROLL):
-            span = range(first, first + UNROLL)
-            wheres = [pos[line_at, at] for at in span]
-            names = [rows[line_at, at] for at in span]
-            values = [spectra[pl.ds(base + at, 1), :] for at in span]
-            for where, name, value in zip(wheres, names, values):
-                placed[pl.ds(where, 1), :] = value
-                tags[where] = name
-
-    @pl.loop(0, les_count)
-    def _(owner):
-        tags[owner * stride + cap] = pos[lines + owner, 0]
-
+    cap = placed.shape[0]
+    rank_rows = cap // GROUPS
+    tag_rows = cap // LANES
     group = lane_group((rank_rows, LANES))
 
-    @pl.loop(0, les_count)
-    def _(owner):
+    def fill(owner):
+        @pl.loop(0, tag_rows)
+        def _(line_at):
+            base = pl.multiple_of(line_at * LANES, LANES)
+            from_line = owner * tag_rows + line_at
+            for first in range(0, LANES, UNROLL):
+                span = range(first, first + UNROLL)
+                ids = [sources[from_line, at] for at in span]
+                values = [spectra[pl.ds(face, 1), :] for face in ids]
+                for at, value in zip(span, values):
+                    placed[pl.ds(base + at, 1), :] = value
+
         total = jnp.zeros((rank_rows, LANES), jnp.float32)
         for part in range(GROUPS):
-            start = pl.multiple_of(owner * stride + part * rank_rows, rank_rows)
-            total = jnp.where(group == part, placed[pl.ds(start, rank_rows), :], total)
-        out[owner] = total
-
-
-def exchange_kernel(
-    les_count, stride, data, tags, data_in, tags_in,
-    data_send, data_recv, tags_send, tags_recv, own_sem, own_tags_sem,
-):
-    les, mode = lax.axis_index("les"), lax.axis_index("modes")
-    barrier = pltpu.get_barrier_semaphore()
-    for step in range(1, les_count):
+            total = jnp.where(group == part, placed[pl.ds(part * rank_rows, rank_rows), :], total)
+        packed[owner, pl.ds(0, rank_rows), :] = total
+        packed[owner, pl.ds(rank_rows, tag_rows), :] = tags[owner]
+
+    def remote(step):
         peer = lax.rem(les + step, les_count)
-        pl.semaphore_signal(barrier, inc=1, device_id=(peer, mode), device_id_type=MESH)
-    own = pltpu.make_async_copy(data.at[les], data_in.at[les], own_sem)
-    own_at = pl.ds(pl.multiple_of(les * stride, stride), stride)
-    own_tags = pltpu.make_async_copy(tags.at[own_at], tags_in.at[own_at], own_tags_sem)
-    own.start()
-    own_tags.start()
-    pl.semaphore_wait(barrier, les_count - 1)
-    copies = []
-    for step in range(1, les_count):
-        peer = lax.rem(les + step, les_count)
-        peer_at = pl.ds(pl.multiple_of(peer * stride, stride), stride)
-        copy = pltpu.make_async_remote_copy(
-            src_ref=tags.at[peer_at],
-            dst_ref=tags_in.at[own_at],
-            send_sem=tags_send.at[step - 1],
-            recv_sem=tags_recv.at[step - 1],
+        return peer, pltpu.make_async_remote_copy(
+            src_ref=packed.at[peer],
+            dst_ref=data_in.at[les],
+            send_sem=send_sem.at[step - 1],
+            recv_sem=recv_sem.at[step - 1],
             device_id=(peer, mode),
             device_id_type=MESH,
         )
+
+    pl.semaphore_wait(barrier, les_count - 1)
+
+    @pl.loop(1, les_count)
+    def _(step):
+        peer, copy = remote(step)
+        fill(peer)
         copy.start()
-        copies.append(copy)
-        copy = pltpu.make_async_remote_copy(
-            src_ref=data.at[peer],
-            dst_ref=data_in.at[les],
-            send_sem=data_send.at[step - 1],
-            recv_sem=data_recv.at[step - 1],
-            device_id=(peer, mode),
-            device_id_type=MESH,
-        )
-        copy.start()
-        copies.append(copy)
+
+    fill(les)
+    own = pltpu.make_async_copy(packed.at[les], data_in.at[les], own_sem)
+    own.start()
     own.wait()
-    own_tags.wait()
-    for copy in copies:
-        copy.wait()
-
-
-def unpack_kernel(cap, stride, tags, data, out, spread, placed):
+
+    @pl.loop(1, les_count)
+    def _(step):
+        remote(step)[1].wait()
+
+
+def unpack_kernel(data, out, spread, placed, name_rows, names, name_sem):
     les_count = data.shape[0]
     mode_count, block_rows, _ = out.shape
     rank_rows = spread.shape[0] // (les_count * GROUPS)
+    cap = rank_rows * GROUPS
+    tag_rows = cap // LANES
+    dump = mode_count * GROUPS * block_rows
+    lines = les_count * tag_rows
+
+    for source in range(les_count):
+        tags = data[source, pl.ds(rank_rows, tag_rows), :]
+        live = jnp.where(tags > 0.0, 1.0, 0.0)
+        live = jnp.sum(jnp.sum(live, axis=0, keepdims=True), axis=1, keepdims=True)
+        live = jnp.broadcast_to(live, (1, LANES)).astype(jnp.int32)
+        found = jnp.where(tags > 0.0, tags - 1.0, float(dump)).astype(jnp.int32)
+        name_rows[source * tag_rows:(source + 1) * tag_rows, :] = found
+        name_rows[lines + source:lines + source + 1, :] = live
+    name_copy = pltpu.make_async_copy(name_rows, names, name_sem)
+    name_copy.start()
+
     @pl.loop(0, les_count)
     def _(source):
         block = data[source, pl.ds(0, rank_rows), :]
@@ -173,28 +204,20 @@
             moved = block if part == 0 else pltpu.roll(block, LANES - part * COLS, 1)
             spread[pl.ds(start, rank_rows), :] = moved
 
-    dump = mode_count * GROUPS * block_rows
+    name_copy.wait()
+    steps_line = LANES // UNROLL
 
     @pl.loop(0, les_count)
     def _(source):
-        live = tags[source * stride + cap]
-
-        @pl.loop(0, live // UNROLL)
+        @pl.loop(0, (names[lines + source, 0] + UNROLL - 1) // UNROLL)
         def _(step):
-            start = pl.multiple_of(step * UNROLL, UNROLL)
-            base = source * cap + start
-            names = [tags[source * stride + start + at] for at in range(UNROLL)]
+            base = pl.multiple_of(source * cap + step * UNROLL, UNROLL)
+            line_at = source * tag_rows + step // steps_line
+            lane_at = (step % steps_line) * UNROLL
+            ids = [names[line_at, lane_at + at] for at in range(UNROLL)]
             values = [spread[pl.ds(base + at, 1), :] for at in range(UNROLL)]
-            for name, value in zip(names, values):
+            for name, value in zip(ids, values):
                 placed[pl.ds(name, 1), :] = value
-
-        @pl.when(live % UNROLL > 0)
-        def _():
-            start = pl.multiple_of(live // UNROLL * UNROLL, UNROLL)
-            base = source * cap + start
-            for at in range(UNROLL):
-                row = jnp.where(start + at < live, tags[source * stride + start + at], dump)
-                placed[pl.ds(row, 1), :] = spread[pl.ds(base + at, 1), :]
 
     group = lane_group((block_rows, LANES))
     halves = GROUPS // 2
@@ -332,7 +355,6 @@
     all_rows = stations * rows_les
     send_cap = face_slots // les_count
     send_total = les_count * send_cap
-    stride = (send_cap // 1024 + 1) * 1024
     lines = face_slots // LANES
     rank_rows = send_cap // GROUPS
     block_rows = stations * point_dev // GROUPS
@@ -340,57 +362,58 @@
     vmem = pl.BlockSpec(memory_space=pltpu.VMEM)
     smem = pl.BlockSpec(memory_space=pltpu.SMEM)
 
-    mode_at = lax.axis_index("modes").astype(jnp.int32).reshape(1)
-
-    packed, tags = pl.pallas_call(
-        functools.partial(pack_kernel, rows_les, send_cap, stride),
+    tag_rows = send_cap // LANES
+    sources, tags = pl.pallas_call(
+        functools.partial(index_kernel, rows_les, les_count),
         out_shape=(
-            jax.ShapeDtypeStruct((les_count, rank_rows, LANES), jnp.float32),
-            jax.ShapeDtypeStruct(((les_count + 1) * stride,), jnp.int32),
+            jax.ShapeDtypeStruct((send_total // LANES, LANES), jnp.int32),
+            jax.ShapeDtypeStruct((send_total // LANES, LANES), jnp.float32),
         ),
-        in_specs=[smem, smem, vmem, vmem, vmem],
-        out_specs=(vmem, smem),
+        in_specs=[smem, vmem],
+        out_specs=(vmem, vmem),
+        scratch_shapes=[pltpu.VMEM((lines, LANES), jnp.int32)] * 2,
+        compiler_params=pltpu.CompilerParams(vmem_limit_bytes=VMEM_BYTES),
+        name="index",
+    )(counts, targets.reshape(lines, LANES))
+
+    peers = les_count - 1
+    data_in = pl.pallas_call(
+        functools.partial(exchange_kernel, les_count, mode_count),
+        out_shape=jax.ShapeDtypeStruct((les_count, rank_rows + tag_rows, LANES), jnp.float32),
+        in_specs=[smem, vmem, vmem, vmem],
+        out_specs=vmem,
         scratch_shapes=[
             pltpu.VMEM((face_slots, LANES), jnp.float32),
-            pltpu.VMEM((les_count * stride + 8, LANES), jnp.float32),
-            pltpu.VMEM((lines + les_count, LANES), jnp.int32),
-            pltpu.SMEM((lines + les_count, LANES), jnp.int32),
-            pltpu.VMEM((lines, LANES), jnp.int32),
-            pltpu.SMEM((lines, LANES), jnp.int32),
-            pltpu.SemaphoreType.DMA,
+            pltpu.VMEM((send_cap, LANES), jnp.float32),
+            pltpu.VMEM((les_count, rank_rows + tag_rows, LANES), jnp.float32),
+            pltpu.SemaphoreType.DMA((peers,)),
+            pltpu.SemaphoreType.DMA((peers,)),
             pltpu.SemaphoreType.DMA,
         ],
-        compiler_params=pltpu.CompilerParams(vmem_limit_bytes=VMEM_BYTES),
-        name="pack",
-    )(counts, mode_at, targets.reshape(lines, LANES), pressure, jnp.asarray(fourier_columns()))
-
-    hbm = pl.BlockSpec(memory_space=pl.ANY)
-    peers = les_count - 1
-    data_in, tags_in = pl.pallas_call(
-        functools.partial(exchange_kernel, les_count, stride),
-        out_shape=(
-            jax.ShapeDtypeStruct((les_count, rank_rows, LANES), jnp.float32),
-            jax.ShapeDtypeStruct((les_count * stride,), jnp.int32),
+        compiler_params=pltpu.CompilerParams(
+            collective_id=1, has_side_effects=True, vmem_limit_bytes=VMEM_BYTES
         ),
-        in_specs=[hbm, hbm],
-        out_specs=(hbm, hbm),
-        scratch_shapes=[pltpu.SemaphoreType.DMA((peers,))] * 4 + [pltpu.SemaphoreType.DMA] * 2,
-        compiler_params=pltpu.CompilerParams(collective_id=1, has_side_effects=True),
         name="exchange",
-    )(packed, tags)
+    )(
+        sources, tags.reshape(les_count, tag_rows, LANES), pressure,
+        jnp.asarray(fourier_columns()),
+    )
 
     blocks = pl.pallas_call(
-        functools.partial(unpack_kernel, send_cap, stride),
+        unpack_kernel,
         out_shape=jax.ShapeDtypeStruct((mode_count, block_rows, LANES), jnp.float32),
-        in_specs=[smem, vmem],
+        in_specs=[vmem],
         out_specs=vmem,
         scratch_shapes=[
             pltpu.VMEM((send_total, LANES), jnp.float32),
             pltpu.VMEM((all_rows + 8, LANES), jnp.float32),
+            pltpu.VMEM((send_total // LANES + les_count, LANES), jnp.int32),
+            pltpu.SMEM((send_total // LANES + les_count, LANES), jnp.int32),
+            pltpu.SemaphoreType.DMA,
         ],
         compiler_params=pltpu.CompilerParams(vmem_limit_bytes=VMEM_BYTES),
         name="unpack",
-    )(tags_in, data_in)
+    )(data_in)
 
     width = mode_total // device_count
     share_rows = (share_form(width)[1] + 7) // 8 * 8

time: 66.6 us -> 63.8 us (0.958); the launches traced: 65.5 us -> 63.5 us
  Pallas kernels: 63.5 us -> 61.5 us
    pallas_call x3, Pallas kernels: 41 us -> 37.2 us  [the longest x1 15.7 us: local(): pl.pallas_call(unpack_kernel, out_shape=jax.ShapeDtypeStruct((mode_count,...]
    pallas_call x1, Pallas kernels: 22.5 us -> 24.3 us  [local(): pl.pallas_call(functools.partial(tail_kernel, les_count, mode_count), out...]
where the time goes in v4:
time: 63.8 us; the launch traced here: 63.5 us
  Pallas kernels  61.5 us (96%)
  local copies, waits for them, and re-layouts  1.32 us (2%)
  between operations  0.68 us (1%)
    pallas_call x1, Pallas kernels, local(): pl.pallas_call(functools.partial(tail_kernel, les_count, mode_count), out...  24.3 us
    pallas_call x1, Pallas kernels, local(): pl.pallas_call(unpack_kernel, out_shape=jax.ShapeDtypeStruct((mode_count,...  15.7 us
    pallas_call x1, Pallas kernels, local(): pl.pallas_call(functools.partial(exchange_kernel, les_count, mode_count),...  15.5 us
    pallas_call x1, Pallas kernels, local(): pl.pallas_call(functools.partial(index_kernel, rows_les, les_count), out_...  6.01 us
    unnamed x1, local copies, waits for them, and re-layouts  1.32 us

profile of v4, /device:TPU:0, one launch (start us, length us, event | category | flops | bytes accessed | tf_op | source)
XLA Modules:
  0.0 63.5 jit_solution(7305871364207377693)
XLA Ops:
  0.7 6.0 %index.1 = (s32[64,128]{1,0:T(8,128)}, f32[64,128]{1,0:T(8,128)}) custom-call(s32[1]{0:T(128)S(6)} %copy.7.counts, s32[64,128]{1,0:T(8,128)} %bitcast.5), custom_call_target="tpu_custom_call" | custom-call | tf_op jit(solution)/shard_map/index/pallas_call | solution.py:366
  6.7 15.5 %exchange.1.data = f32[8,136,128]{2,1,0:T(8,128)} custom-call(s32[64,128]{1,0:T(8,128)} %get-tuple-element.7.sources, f32[8,8,128]{2,1,0:T(8,128)} %bitcast.4, bf16[8192,128]{1,0:T(8,128)(2,1)} %pressure.1, bf16[2,512,128]{2,1,0:T(8,128)(2,1)} %constant.2.clone.basis), custom_call_target="tpu_custom_call" | custom-call | tf_op jit(solution)/shard_map/exchange/pallas_call | solution.py:380
  22.1 15.7 %unpack.1.blocks = f32[4,128,128]{2,1,0:T(8,128)} custom-call(f32[8,136,128]{2,1,0:T(8,128)} %exchange.1.data), custom_call_target="tpu_custom_call" | custom-call | tf_op jit(solution)/shard_map/unpack/pallas_call | solution.py:402
  37.8 24.3 %tail.1 = f32[2,16,48]{2,1,0:T(8,128)} custom-call(f32[4,128,128]{2,1,0:T(8,128)} %unpack.1.blocks, bf16[2,1536,512]{2,1,0:T(8,128)(2,1)} %pinv.1), custom_call_target="tpu_custom_call" | custom-call | tf_op jit(solution)/shard_map/tail/pallas_call | solution.py:420
  62.2 1.3 %copy.8 = f32[2,2,8,48]{3,2,1,0:T(8,128)} copy(f32[2,2,8,48]{3,2,1,0:T(8,128)} %bitcast.3) | data formatting | bytes 12288

commit v5 on v4

--- a/solution.py
+++ b/solution.py
@@ -104,23 +104,31 @@
 
 def exchange_kernel(
     les_count, mode_count, sources, tags, pressure, basis, data_in,
-    spectra, placed, packed, send_sem, recv_sem, own_sem,
+    samples, spectra, placed, packed, load_sem, send_sem, recv_sem, own_sem,
 ):
     les, mode = lax.axis_index("les"), lax.axis_index("modes")
+    face_slots, block_len = pressure.shape
+    chunk = math.gcd(face_slots, 1024)
+
+    def load(step):
+        at = pl.ds(pl.multiple_of(step * chunk, chunk), chunk)
+        return pltpu.make_async_copy(pressure.at[at], samples.at[at], load_sem.at[step])
+
+    for step in range(face_slots // chunk):
+        load(step).start()
     barrier = pltpu.get_barrier_semaphore()
     for step in range(1, les_count):
         peer = lax.rem(les + step, les_count)
         pl.semaphore_signal(barrier, inc=1, device_id=(peer, mode), device_id_type=MESH)
 
-    face_slots, block_len = pressure.shape
-    chunk = math.gcd(face_slots, 1024)
     times = pl.ds(pl.multiple_of(mode * block_len, block_len), block_len)
     block_basis = jnp.concatenate([basis[0, times, :], basis[1, times, :]], axis=0)
 
     @pl.loop(0, face_slots // chunk)
     def _(step):
         at = pl.ds(pl.multiple_of(step * chunk, chunk), chunk)
-        block = pressure[at, :]
+        load(step).wait()
+        block = samples[at, :]
         block = jnp.concatenate([block, block], axis=1)
         spectra[at, :] = jnp.dot(block, block_basis, preferred_element_type=jnp.float32)
 
@@ -205,19 +213,25 @@
             spread[pl.ds(start, rank_rows), :] = moved
 
     name_copy.wait()
-    steps_line = LANES // UNROLL
 
     @pl.loop(0, les_count)
     def _(source):
-        @pl.loop(0, (names[lines + source, 0] + UNROLL - 1) // UNROLL)
-        def _(step):
-            base = pl.multiple_of(source * cap + step * UNROLL, UNROLL)
-            line_at = source * tag_rows + step // steps_line
-            lane_at = (step % steps_line) * UNROLL
-            ids = [names[line_at, lane_at + at] for at in range(UNROLL)]
-            values = [spread[pl.ds(base + at, 1), :] for at in range(UNROLL)]
-            for name, value in zip(ids, values):
-                placed[pl.ds(name, 1), :] = value
+        live = names[lines + source, 0]
+
+        @pl.loop(0, (live + LANES - 1) // LANES)
+        def _(part):
+            line_at = source * tag_rows + part
+            base = pl.multiple_of(line_at * LANES, LANES)
+            for first in range(0, LANES, 2 * UNROLL):
+
+                @pl.when(part * LANES + first < live)
+                def _(first=first):
+                    for begin in range(first, first + 2 * UNROLL, UNROLL):
+                        span = range(begin, begin + UNROLL)
+                        ids = [names[line_at, at] for at in span]
+                        values = [spread[pl.ds(base + at, 1), :] for at in span]
+                        for name, value in zip(ids, values):
+                            placed[pl.ds(name, 1), :] = value
 
     group = lane_group((block_rows, LANES))
     halves = GROUPS // 2
@@ -380,12 +394,14 @@
     data_in = pl.pallas_call(
         functools.partial(exchange_kernel, les_count, mode_count),
         out_shape=jax.ShapeDtypeStruct((les_count, rank_rows + tag_rows, LANES), jnp.float32),
-        in_specs=[smem, vmem, vmem, vmem],
+        in_specs=[smem, vmem, pl.BlockSpec(memory_space=pl.ANY), vmem],
         out_specs=vmem,
         scratch_shapes=[
+            pltpu.VMEM(pressure.shape, pressure.dtype),
             pltpu.VMEM((face_slots, LANES), jnp.float32),
             pltpu.VMEM((send_cap, LANES), jnp.float32),
             pltpu.VMEM((les_count, rank_rows + tag_rows, LANES), jnp.float32),
+            pltpu.SemaphoreType.DMA((face_slots // math.gcd(face_slots, 1024),)),
             pltpu.SemaphoreType.DMA((peers,)),
             pltpu.SemaphoreType.DMA((peers,)),
             pltpu.SemaphoreType.DMA,

time: 63.8 us -> 57 us (0.89)
  Pallas kernels: 61.5 us -> 54.7 us
    pallas_call x1, Pallas kernels: 15.7 us -> 8.37 us  [local(): pl.pallas_call(unpack_kernel, out_shape=jax.ShapeDtypeStruct((mode_count,...]
where the time goes in v5:
time: 57 us; the launch traced here: 56.7 us
  Pallas kernels  54.7 us (96%)
  local copies, waits for them, and re-layouts  1.32 us (2%)
  between operations  0.68 us (1%)
    pallas_call x1, Pallas kernels, local(): pl.pallas_call(functools.partial(tail_kernel, les_count, mode_count), out...  24.3 us
    pallas_call x1, Pallas kernels, local(): pl.pallas_call(functools.partial(exchange_kernel, les_count, mode_count),...  16 us
    pallas_call x1, Pallas kernels, local(): pl.pallas_call(unpack_kernel, out_shape=jax.ShapeDtypeStruct((mode_count,...  8.37 us
    pallas_call x1, Pallas kernels, local(): pl.pallas_call(functools.partial(index_kernel, rows_les, les_count), out_...  6.01 us
    unnamed x1, local copies, waits for them, and re-layouts  1.32 us

profile of v5, /device:TPU:0, one launch (start us, length us, event | category | flops | bytes accessed | tf_op | source)
XLA Modules:
  0.0 56.7 jit_solution(2297624093488519328)
XLA Ops:
  0.7 6.0 %index.1 = (s32[64,128]{1,0:T(8,128)}, f32[64,128]{1,0:T(8,128)}) custom-call(s32[1]{0:T(128)S(6)} %copy.7.counts, s32[64,128]{1,0:T(8,128)} %bitcast.5), custom_call_target="tpu_custom_call" | custom-call | tf_op jit(solution)/shard_map/index/pallas_call | solution.py:380
  6.7 16.0 %exchange.1.data = f32[8,136,128]{2,1,0:T(8,128)} custom-call(s32[64,128]{1,0:T(8,128)} %get-tuple-element.7.sources, f32[8,8,128]{2,1,0:T(8,128)} %bitcast.4, bf16[8192,128]{1,0:T(8,128)(2,1)} %pressure.1, bf16[2,512,128]{2,1,0:T(8,128)(2,1)} %constant.2.clone.basis), custom_call_target="tpu_custom_call" | custom-call | tf_op jit(solution)/shard_map/exchange/pallas_call | solution.py:394
  22.7 8.4 %unpack.1.blocks = f32[4,128,128]{2,1,0:T(8,128)} custom-call(f32[8,136,128]{2,1,0:T(8,128)} %exchange.1.data), custom_call_target="tpu_custom_call" | custom-call | tf_op jit(solution)/shard_map/unpack/pallas_call | solution.py:418
  31.0 24.3 %tail.1 = f32[2,16,48]{2,1,0:T(8,128)} custom-call(f32[4,128,128]{2,1,0:T(8,128)} %unpack.1.blocks, bf16[2,1536,512]{2,1,0:T(8,128)(2,1)} %pinv.1), custom_call_target="tpu_custom_call" | custom-call | tf_op jit(solution)/shard_map/tail/pallas_call | solution.py:436
  55.3 1.3 %copy.8 = f32[2,2,8,48]{3,2,1,0:T(8,128)} copy(f32[2,2,8,48]{3,2,1,0:T(8,128)} %bitcast.3) | data formatting | bytes 12288

commit v6 on v5

--- a/solution.py
+++ b/solution.py
@@ -104,18 +104,12 @@
 
 def exchange_kernel(
     les_count, mode_count, sources, tags, pressure, basis, data_in,
-    samples, spectra, placed, packed, load_sem, send_sem, recv_sem, own_sem,
+    spectra, placed, packed, send_sem, recv_sem, own_sem,
 ):
     les, mode = lax.axis_index("les"), lax.axis_index("modes")
     face_slots, block_len = pressure.shape
     chunk = math.gcd(face_slots, 1024)
 
-    def load(step):
-        at = pl.ds(pl.multiple_of(step * chunk, chunk), chunk)
-        return pltpu.make_async_copy(pressure.at[at], samples.at[at], load_sem.at[step])
-
-    for step in range(face_slots // chunk):
-        load(step).start()
     barrier = pltpu.get_barrier_semaphore()
     for step in range(1, les_count):
         peer = lax.rem(les + step, les_count)
@@ -127,8 +121,7 @@
     @pl.loop(0, face_slots // chunk)
     def _(step):
         at = pl.ds(pl.multiple_of(step * chunk, chunk), chunk)
-        load(step).wait()
-        block = samples[at, :]
+        block = pressure[at, :]
         block = jnp.concatenate([block, block], axis=1)
         spectra[at, :] = jnp.dot(block, block_basis, preferred_element_type=jnp.float32)
 
@@ -394,14 +387,12 @@
     data_in = pl.pallas_call(
         functools.partial(exchange_kernel, les_count, mode_count),
         out_shape=jax.ShapeDtypeStruct((les_count, rank_rows + tag_rows, LANES), jnp.float32),
-        in_specs=[smem, vmem, pl.BlockSpec(memory_space=pl.ANY), vmem],
+        in_specs=[smem, vmem, vmem, vmem],
         out_specs=vmem,
         scratch_shapes=[
-            pltpu.VMEM(pressure.shape, pressure.dtype),
             pltpu.VMEM((face_slots, LANES), jnp.float32),
             pltpu.VMEM((send_cap, LANES), jnp.float32),
             pltpu.VMEM((les_count, rank_rows + tag_rows, LANES), jnp.float32),
-            pltpu.SemaphoreType.DMA((face_slots // math.gcd(face_slots, 1024),)),
             pltpu.SemaphoreType.DMA((peers,)),
             pltpu.SemaphoreType.DMA((peers,)),
             pltpu.SemaphoreType.DMA,

time: 57 us -> 56.5 us (level)
  Pallas kernels: 54.7 us -> 54.1 us
where the time goes in v6:
time: 56.5 us; the launch traced here: 56.1 us
  Pallas kernels  54.1 us (96%)
  local copies, waits for them, and re-layouts  1.32 us (2%)
  between operations  0.68 us (1%)
    pallas_call x1, Pallas kernels, local(): pl.pallas_call(functools.partial(tail_kernel, les_count, mode_count), out...  24.3 us
    pallas_call x1, Pallas kernels, local(): pl.pallas_call(functools.partial(exchange_kernel, les_count, mode_count),...  15.5 us
    pallas_call x1, Pallas kernels, local(): pl.pallas_call(unpack_kernel, out_shape=jax.ShapeDtypeStruct((mode_count,...  8.37 us
    pallas_call x1, Pallas kernels, local(): pl.pallas_call(functools.partial(index_kernel, rows_les, les_count), out_...  6.01 us
    unnamed x1, local copies, waits for them, and re-layouts  1.32 us

profile of v6, /device:TPU:0, one launch (start us, length us, event | category | flops | bytes accessed | tf_op | source)
XLA Modules:
  0.0 56.1 jit_solution(607303746677816273)
XLA Ops:
  0.7 6.0 %index.1 = (s32[64,128]{1,0:T(8,128)}, f32[64,128]{1,0:T(8,128)}) custom-call(s32[1]{0:T(128)S(6)} %copy.7.counts, s32[64,128]{1,0:T(8,128)} %bitcast.5), custom_call_target="tpu_custom_call" | custom-call | tf_op jit(solution)/shard_map/index/pallas_call | solution.py:373
  6.7 15.5 %exchange.1.data = f32[8,136,128]{2,1,0:T(8,128)} custom-call(s32[64,128]{1,0:T(8,128)} %get-tuple-element.7.sources, f32[8,8,128]{2,1,0:T(8,128)} %bitcast.4, bf16[8192,128]{1,0:T(8,128)(2,1)} %pressure.1, bf16[2,512,128]{2,1,0:T(8,128)(2,1)} %constant.2.clone.basis), custom_call_target="tpu_custom_call" | custom-call | tf_op jit(solution)/shard_map/exchange/pallas_call | solution.py:387
  22.1 8.4 %unpack.1.blocks = f32[4,128,128]{2,1,0:T(8,128)} custom-call(f32[8,136,128]{2,1,0:T(8,128)} %exchange.1.data), custom_call_target="tpu_custom_call" | custom-call | tf_op jit(solution)/shard_map/unpack/pallas_call | solution.py:409
  30.5 24.3 %tail.1 = f32[2,16,48]{2,1,0:T(8,128)} custom-call(f32[4,128,128]{2,1,0:T(8,128)} %unpack.1.blocks, bf16[2,1536,512]{2,1,0:T(8,128)(2,1)} %pinv.1), custom_call_target="tpu_custom_call" | custom-call | tf_op jit(solution)/shard_map/tail/pallas_call | solution.py:427
  54.8 1.3 %copy.8 = f32[2,2,8,48]{3,2,1,0:T(8,128)} copy(f32[2,2,8,48]{3,2,1,0:T(8,128)} %bitcast.3) | data formatting | bytes 12288
